TPU v7x, 32 devices: a whole 2x2x4 slice. The times are simulated.
32 devices in a mesh: parts: 2 (over y), ctx: 4 (over z), opt: 4 (over x, core).
Axes of the slice: x: 2, y: 2, z: 4, core: 2. Of those that a mesh axis runs over, the one named last changes fastest.
Arguments:
- options: bfloat16 [8, 32, 3072], P(('parts', 'opt'), 'ctx'), parts along dimension 0, may hold values from -6 to 6
- cache_keys: bfloat16 [1024, 512], P(('parts', 'ctx')), parts along dimension 0, may hold values from -800 to 800
- cache_values: bfloat16 [1024, 512], P(('parts', 'ctx')), parts along dimension 0, may hold values from -6 to 6
- attention_gain: float32 [3072], replicated, may hold values from 0.5 to 1.5
- expert_gain: float32 [3072], replicated, may hold values from 0.5 to 1.5
- input_weight: bfloat16 [3072, 4096], P(None, 'ctx'), may hold values from -0.109375 to 0.109375
- output_weight: bfloat16 [3072, 3072], P(None, 'ctx'), may hold values from -0.875 to 0.875
- router_weight: bfloat16 [3072, 8], replicated, may hold values from -0.109375 to 0.109375
- gate_weight: bfloat16 [3072, 65536], P(None, ('ctx', 'opt')), may hold values from -0.109375 to 0.109375
- up_weight: bfloat16 [3072, 65536], P(None, ('ctx', 'opt')), may hold values from -0.109375 to 0.109375
- down_weight: bfloat16 [65536, 3072], P(('ctx', 'opt')), may hold values from -0.0625 to 0.0625
- routing: int32 [8, 32, 2], P(('parts', 'opt'), 'ctx'), parts along dimension 0, may hold values from 0 to 7, all different within a row; in each aligned block of 8 rows (0 to 7, 8 to 15, ..., all dimensions but the last counted through in order) at most 4 rows name the same one
Outputs:
- layer_out: bfloat16 [8, 32, 3072], P(('parts', 'opt'), 'ctx'), parts along dimension 0
There are 2 independent parts, one for each index of `parts`. A program takes and returns all parts, laid end to end along the dimension named above; an argument that names none is the same for every part. Nothing has to cross between parts.
Inputs may be any that keep to these rules, and one draw needn't show every extreme that they name: `routing`: at most 4 of the 8 rows of one device name the same expert, and in some device one expert is named by exactly 4 rows; the two experts of a row differ.
All inputs are finite; a program needn't handle non-finite values.
Results may differ from a plain program's by a relative error of at most 0.018.
Values may be sent and summed in bfloat16 or wider, within the bound.
No kernel may reach another device: no remote copies, remote signals or barrier semaphores. Data moves between devices by JAX's collectives and lax.ppermute only.
A program may use at most 192 MiB of HBM per device.

v0:
```python
import jax
import jax.numpy as jnp
from jax import lax
from jax.experimental import pallas as pl
from jax.experimental.pallas import tpu as pltpu
from jax.sharding import PartitionSpec as P


H = 24
KVH = 4
HD = 128
FF = 8192
MOST = 4


EPS = 1e-05
THETA = 1000000.0


def combined_all(x, axis, combine):
    everything = jax.tree.map(
        lambda part, kind: lax.all_gather(part.astype(kind), axis),
        x,
        (jnp.bfloat16, jnp.bfloat16, jnp.bfloat16),
    )

    def take(k):
        return jax.tree.map(lambda part, own: part[k].astype(own.dtype), everything, x)

    return lax.fori_loop(
        1, lax.axis_size(axis), lambda k, so_far: combine(so_far, take(k)), take(0)
    )


def rms_scale(row_data, gain_vector):
    floats = row_data.astype(jnp.float32)
    factor = lax.rsqrt(jnp.mean(floats * floats, axis=-1, keepdims=True) + EPS)
    return (floats * factor * gain_vector).astype(jnp.bfloat16)


def rotate(tile_data, first_head, positions):
    row_count, tile_width = tile_data.shape
    head_count = tile_width // HD
    half_dim = HD // 2
    split_view = tile_data.reshape(row_count, head_count, 2, half_dim)
    inverse = THETA ** (-2.0 * jnp.arange(half_dim, dtype=jnp.float32) / HD)
    angles = positions.astype(jnp.float32)[:, None] * inverse[None, :]
    cosine = jnp.cos(angles)[:, None, :]
    sine_part = jnp.sin(angles)[:, None, :]
    lower_half = split_view[:, :, 0]
    upper_half = split_view[:, :, 1]
    turned = jnp.stack(
        [
            lower_half * cosine - upper_half * sine_part,
            upper_half * cosine + lower_half * sine_part,
        ],
        axis=2,
    )
    rotated_head = first_head + jnp.arange(head_count) < H + KVH
    return jnp.where(rotated_head[None, :, None, None], turned, split_view).reshape(
        row_count, tile_width
    )


def softmax_parts(queries, key_rows, value_rows, key_start, cached):
    key_count = key_rows.shape[0]
    key_heads = key_rows.reshape(key_count, KVH, HD)
    value_heads = value_rows.reshape(key_count, KVH, HD).astype(jnp.float32)
    scores = jnp.einsum(
        "rhgd,khd->hgrk", queries, key_heads, preferred_element_type=jnp.float32
    ) * HD ** (-0.5)
    query_index = jnp.arange(queries.shape[0])
    key_index = jnp.arange(key_count)
    visible = (key_index[None, :] < cached) | (
        key_start + key_index[None, :] - cached <= query_index[:, None]
    )
    scores = jnp.where(visible, scores, -jnp.inf)
    maxima = jnp.max(scores, axis=-1)
    weights = jnp.exp(scores - maxima[..., None])
    totals = jnp.sum(weights, axis=-1)
    summed = jnp.einsum("hgrk,khd->hgrd", weights, value_heads, precision=lax.Precision.HIGHEST)
    return (maxima, totals, summed)


def join_parts(first, second):
    first_max, first_total, first_sum = first
    second_max, second_total, second_sum = second
    larger = jnp.maximum(first_max, second_max)
    first_scale = jnp.exp(first_max - larger)
    second_scale = jnp.exp(second_max - larger)
    return (
        larger,
        first_total * first_scale + second_total * second_scale,
        first_sum * first_scale[..., None] + second_sum * second_scale[..., None],
    )


def general_shards(
    options,
    cache_keys,
    cache_values,
    attention_gain,
    expert_gain,
    input_weight,
    output_weight,
    router_weight,
    gate_weight,
    up_weight,
    down_weight,
    routing,
):
    own_rows = options[0]
    ctx_count = lax.axis_size("ctx")
    ctx_here = lax.axis_index("ctx")
    local_rows = own_rows.shape[0]
    passage = cache_keys.shape[0] * ctx_count
    tile_columns = input_weight.shape[1]
    first_head = ctx_here * (tile_columns // HD)
    normed = rms_scale(own_rows, attention_gain)
    row_piece = lax.all_gather(normed, "ctx", axis=0, tiled=True)
    product = jnp.dot(row_piece, input_weight, preferred_element_type=jnp.float32)
    where_at = passage + jnp.int32(0) + jnp.arange(row_piece.shape[0])
    rotated_tile = rotate(product, first_head, where_at).astype(jnp.bfloat16)
    projected = lax.all_gather(rotated_tile, "ctx", axis=1, tiled=True)
    option_len = projected.shape[0]
    query_width = H * HD
    key_end = (H + KVH) * HD
    queries = projected[:, :query_width].reshape(option_len, KVH, H // KVH, HD)
    option_keys = projected[:, query_width:key_end]
    option_values = projected[:, key_end:]
    own_start = ctx_here * local_rows
    own_keys = lax.dynamic_slice_in_dim(option_keys, own_start, local_rows, 0)
    own_values = lax.dynamic_slice_in_dim(option_values, own_start, local_rows, 0)
    key_rows = jnp.concatenate([cache_keys, own_keys], axis=0)
    value_rows = jnp.concatenate([cache_values, own_values], axis=0)
    local_max, local_total, local_sum = softmax_parts(
        queries, key_rows, value_rows, own_start, cache_keys.shape[0]
    )
    _, totals, summed = combined_all((local_max, local_total, local_sum), "ctx", join_parts)
    attention = (
        (summed / totals[..., None])
        .transpose(2, 0, 1, 3)
        .reshape(option_len, query_width)
        .astype(jnp.bfloat16)
    )
    columns = jnp.dot(attention, output_weight, preferred_element_type=jnp.float32).astype(
        jnp.bfloat16
    )
    attention_out = lax.all_to_all(columns, "ctx", split_axis=0, concat_axis=1, tiled=True)
    mixed_in = (own_rows.astype(jnp.float32) + attention_out.astype(jnp.float32)).astype(
        jnp.bfloat16
    )
    expert_in = rms_scale(mixed_in, expert_gain)
    chosen_ids = routing[0]
    top_count = chosen_ids.shape[1]
    expert_count = router_weight.shape[1]
    logits = jnp.dot(expert_in, router_weight, preferred_element_type=jnp.float32)
    matches = chosen_ids[:, :, None] == jnp.arange(expert_count)[None, None, :]
    picked = jnp.sum(jnp.where(matches, logits[:, None, :], 0.0), axis=-1)
    gate_share = jax.nn.softmax(picked, axis=-1)
    ctx_width = expert_count * FF // ctx_count
    first_target = chosen_ids * FF // ctx_width
    last_target = ((chosen_ids + 1) * FF - 1) // ctx_width
    destination = jnp.arange(ctx_count)
    goes_to = (destination[None, None, :] >= first_target[:, :, None]) & (
        destination[None, None, :] <= last_target[:, :, None]
    )
    flat_goes = goes_to.reshape(local_rows * top_count, ctx_count).astype(jnp.int32)
    slot_index = jnp.cumsum(flat_goes, axis=0) - flat_goes
    slot_count = MOST * max(1, expert_count // ctx_count)
    slot_match = (flat_goes[:, :, None] == 1) & (
        slot_index[:, :, None] == jnp.arange(slot_count)[None, None, :]
    )
    slot_match = slot_match.reshape(local_rows, top_count, ctx_count * slot_count)
    token_slots = jnp.any(slot_match, axis=1).astype(jnp.bfloat16)
    model_width = expert_in.shape[1]
    outgoing = jnp.einsum(
        "rs,rd->sd", token_slots, expert_in, preferred_element_type=jnp.float32
    ).astype(jnp.bfloat16)
    outgoing = outgoing.reshape(ctx_count, slot_count, model_width)
    outgoing_ids = jnp.sum(jnp.where(slot_match, chosen_ids[:, :, None] + 1, 0), axis=(0, 1)) - 1
    outgoing_ids = outgoing_ids.reshape(ctx_count, slot_count)
    arrived, arrived_ids = (
        lax.all_to_all(outgoing, "ctx", split_axis=0, concat_axis=0, tiled=True),
        lax.all_to_all(outgoing_ids, "ctx", split_axis=0, concat_axis=0, tiled=True),
    )
    pooled, pooled_ids = (
        lax.all_gather(arrived, "opt", axis=0, tiled=True),
        lax.all_gather(arrived_ids, "opt", axis=0, tiled=True),
    )
    pooled = pooled.reshape(-1, model_width)
    pooled_ids = pooled_ids.reshape(-1)
    local_width = gate_weight.shape[1]
    opt_count = lax.axis_size("opt")
    column_start = (ctx_here * opt_count + lax.axis_index("opt")) * local_width
    column_expert = (column_start + jnp.arange(local_width)) // FF
    owned_mask = pooled_ids[:, None] == column_expert[None, :]
    gate_part = jnp.dot(pooled, gate_weight, preferred_element_type=jnp.float32)
    up_part = jnp.dot(pooled, up_weight, preferred_element_type=jnp.float32)
    hidden = jnp.where(owned_mask, jax.nn.silu(gate_part) * up_part, 0.0).astype(jnp.bfloat16)
    partial_out = jnp.dot(hidden, down_weight, preferred_element_type=jnp.float32)
    summed_back = lax.psum_scatter(
        partial_out.astype(jnp.bfloat16), "opt", scatter_dimension=0, tiled=True
    ).astype(jnp.float32)
    returned = lax.all_to_all(
        summed_back.reshape(ctx_count, slot_count, model_width).astype(jnp.bfloat16),
        "ctx",
        split_axis=0,
        concat_axis=0,
        tiled=True,
    ).astype(jnp.float32)
    weighting = jnp.sum(jnp.where(slot_match, gate_share[:, :, None], 0.0), axis=1)
    expert_sum = jnp.dot(
        weighting,
        returned.reshape(-1, model_width),
        precision=lax.Precision.HIGHEST,
        preferred_element_type=jnp.float32,
    )
    layer_out = (mixed_in.astype(jnp.float32) + expert_sum).astype(jnp.bfloat16)
    return layer_out[None]


def whole():
    return pl.BlockSpec(memory_space=pltpu.VMEM)


def anywhere():
    return pl.BlockSpec(memory_space=pl.ANY)


def kept(x):
    return pltpu.with_memory_space_constraint(x, pltpu.VMEM)


def flip(x, axis, mask):
    return lax.ppermute(x, axis, [(i, i ^ mask) for i in range(lax.axis_size(axis))])


def gathered(x, axis):
    masks = range(lax.axis_size(axis) - 1, 0, -1)
    return [x] + [flip(x, axis, mask) for mask in masks][::-1]


def aligned(index, size):
    return pl.ds(pl.multiple_of(index * size, size), size)


def cost(flops=0, bytes_accessed=0, transcendentals=0):
    return pl.CostEstimate(
        flops=flops, bytes_accessed=bytes_accessed, transcendentals=transcendentals
    )


def staged():
    return cost(flops=STAGE_FLOPS)


def params(limit):
    return pltpu.CompilerParams(vmem_limit_bytes=limit)


MIB = 1 << 20
STAGE_FLOPS = 8 * 10**9
HEADS_ORDER = (1, 2, 3)
EXPERT_MIB = 11


class Tiles:
    def __init__(self, source, buffers, sems):
        self.source, self.buffers, self.sems = source, buffers, sems
        self.slots, _, self.width = buffers.shape
        self.count = source.shape[1] // self.width

    def copy(self, i):
        slot = i % self.slots
        return pltpu.make_async_copy(
            self.source.at[:, pl.ds(i * self.width, self.width)],
            self.buffers.at[slot],
            self.sems.at[slot],
        )

    def start(self, i):
        if i < self.count:
            self.copy(i).start()

    def open(self):
        for i in range(self.slots):
            self.start(i)

    def ready(self, i):
        self.copy(i).wait()
        return self.buffers[i % self.slots]


def head_plan(ctx_count, tile_heads):
    per = H // ctx_count
    wanted = [
        [per * c + i for i in range(per)] + [H + c, H + KVH + c] for c in range(ctx_count)
    ]
    sends = {}
    for dst in range(ctx_count):
        for head in wanted[dst]:
            sends.setdefault((head // tile_heads, dst), []).append(head)
    pairs = {}
    for shift in range(1, ctx_count):
        found = [(s, (s + shift) % ctx_count) for s in range(ctx_count)]
        found = [pair for pair in found if pair in sends]
        if found:
            pairs[shift] = found
    return wanted, sends, pairs


def tables(cosine, sine):
    def kernel(cosine_ref, sine_ref, cosine_out, sine_out):
        cosine_out[...] = cosine_ref[...]
        sine_out[...] = sine_ref[...]

    return pl.pallas_call(
        kernel,
        out_shape=[jax.ShapeDtypeStruct(cosine.shape, cosine.dtype)] * 2,
        in_specs=[whole()] * 2,
        out_specs=[whole()] * 2,
        compiler_params=params(2 * MIB),
        cost_estimate=staged(),
        name="tables",
    )(cosine, sine)


def pack(cache_keys, cache_values, routing, after):
    passage_rows = cache_keys.shape[0]
    top_count, rows = routing.shape
    half = passage_rows // 2

    def kernel(keys_ref, values_ref, routing_ref, after_ref, *refs):
        out_refs, ids_ref = refs[:-1], refs[-1]
        here = lax.axis_index("ctx")
        core = lax.axis_index("opt") % 2
        row = lax.broadcasted_iota(jnp.int32, (rows, rows), 0)
        column = lax.broadcasted_iota(jnp.int32, (rows, rows), 1)
        lane = lax.broadcasted_iota(jnp.int32, (rows, HD), 1)
        numbers = jnp.zeros((rows, HD), jnp.float32)
        for k in range(top_count):
            spread = jnp.where(row == column, routing_ref[k : k + 1, :].astype(jnp.float32), 0.0)
            numbers = numbers + jnp.where(lane == k, jnp.sum(spread, axis=1, keepdims=True), 0.0)
        for ref, who in zip(out_refs, (here, here ^ (1 + core), here ^ 3)):
            count = ref.shape[0]
            start = 0 if count == passage_rows else pl.multiple_of(core * half, half)
            for side, source in enumerate((keys_ref, values_ref)):
                ref[:, side * HD : (side + 1) * HD] = source[pl.ds(start, count), aligned(who, HD)]
        ids_ref[...] = numbers.astype(jnp.bfloat16)

    return pl.pallas_call(
        kernel,
        out_shape=[
            jax.ShapeDtypeStruct((count, 2 * HD), jnp.bfloat16)
            for count in (passage_rows, passage_rows, half)
        ]
        + [jax.ShapeDtypeStruct((rows, HD), jnp.bfloat16)],
        in_specs=[whole()] * 3 + [anywhere()],
        out_specs=[whole()] * 4,
        compiler_params=params(4 * MIB),
        cost_estimate=staged(),
        name="pack",
    )(cache_keys, cache_values, routing, after)


def project(parts, gain, weight, cosine, sine, plan):
    rows, width = parts[0].shape
    ctx_count = len(parts)
    total, columns = rows * ctx_count, weight.shape[1]
    heads = columns // HD
    _, sends, pairs = plan
    shifts = sorted(pairs)
    widths = [max(len(sends[pair]) for pair in pairs[shift]) * HD for shift in shifts]
    step = 4 * HD

    def kernel(*refs):
        part_refs = refs[:ctx_count]
        gain_ref, weight_ref, cosine_ref, sine_ref, tile_ref = refs[ctx_count : ctx_count + 5]
        payload_refs, normed_ref = refs[ctx_count + 5 : -1], refs[-1]
        here = lax.axis_index("ctx")
        for k in range(ctx_count):
            floats = part_refs[k][...].astype(jnp.float32)
            factor = lax.rsqrt(jnp.mean(floats * floats, axis=-1, keepdims=True) + EPS)
            normed_ref[aligned(here ^ k, rows), :] = floats * factor * gain_ref[...]
        normed = normed_ref[...].astype(jnp.bfloat16)
        for i in range(columns // step):
            product = jnp.dot(
                normed, weight_ref[:, i * step : (i + 1) * step], preferred_element_type=jnp.float32
            )
            for at in range(0, step, HD):
                head = (i * step + at) // HD
                plain = product[:, at : at + HD]
                turned = plain * cosine_ref[...] + pltpu.roll(plain, HD // 2, 1) * sine_ref[...]
                turned = jnp.where(here * heads + head < H + KVH, turned, plain)
                tile_ref[:, head * HD : (head + 1) * HD] = turned.astype(jnp.bfloat16)
        for s in range(ctx_count):

            @pl.when(here == s)
            def _():
                for shift, payload_ref in zip(shifts, payload_refs):
                    for place, head in enumerate(sends.get((s, (s + shift) % ctx_count), [])):
                        local = (head - s * heads) * HD
                        payload_ref[:, place * HD : (place + 1) * HD] = tile_ref[:, local : local + HD]

    out = pl.pallas_call(
        kernel,
        out_shape=[jax.ShapeDtypeStruct((total, n), jnp.bfloat16) for n in [columns] + widths],
        in_specs=[whole()] * (ctx_count + 4),
        out_specs=[whole()] * (1 + len(shifts)),
        scratch_shapes=[pltpu.VMEM((total, width), jnp.float32)],
        compiler_params=params(4 * MIB),
        cost_estimate=cost(bytes_accessed=2 * width * columns),
        name="project",
    )(*parts, gain[None], kept(weight), cosine, sine)
    return out[0], dict(zip(shifts, out[1:]))


def attend(tile, arrived, passage_parts, ids, plan):
    total, rows = tile.shape[0], ids.shape[0]
    ctx_count = lax.axis_size("ctx")
    heads = tile.shape[1] // HD
    wanted, sends, _ = plan
    group = len(wanted[0]) - 2
    shifts = sorted(arrived)

    def kernel(*refs):
        tile_ref = refs[0]
        arrived_refs = dict(zip(shifts, refs[1 : 1 + len(shifts)]))
        passage_refs = refs[1 + len(shifts) : -3]
        numbers_ref, out_ref, mine_ref = refs[-3:]
        here = lax.axis_index("ctx")
        for dst in range(ctx_count):

            @pl.when(here == dst)
            def _():
                for place, head in enumerate(wanted[dst]):
                    src = head // heads
                    if src == dst:
                        block, at = tile_ref, head - src * heads
                    else:
                        block = arrived_refs[(dst - src) % ctx_count]
                        at = sends[(src, dst)].index(head)
                    mine_ref[:, place * HD : (place + 1) * HD] = block[:, at * HD : (at + 1) * HD]

        def part(place):
            return mine_ref[:, place * HD : (place + 1) * HD]

        queries = jnp.concatenate([part(place) for place in range(group)], axis=0)
        keys = [ref[:, :HD] for ref in passage_refs] + [part(group)]
        values = [ref[:, HD:] for ref in passage_refs] + [part(group + 1)]
        scores = []
        for block in keys:
            scores.append(
                lax.dot_general(
                    queries, block, (((1,), (1,)), ((), ())), preferred_element_type=jnp.float32
                )
                * HD ** (-0.5)
            )
        token = lax.broadcasted_iota(jnp.int32, (total, total), 0)
        key = lax.broadcasted_iota(jnp.int32, (total, total), 1)
        bias = jnp.where(key <= token, 0.0, -jnp.inf)
        scores[-1] = scores[-1] + jnp.concatenate([bias] * group, axis=0)
        maxima = jnp.max(scores[0], axis=-1, keepdims=True)
        for block in scores[1:]:
            maxima = jnp.maximum(maxima, jnp.max(block, axis=-1, keepdims=True))
        sums, totals = 0.0, 0.0
        for block, value in zip(scores, values):
            weights = jnp.exp(block - maxima)
            totals = totals + jnp.sum(weights, axis=-1, keepdims=True)
            high = weights.astype(jnp.bfloat16)
            low = (weights - high.astype(jnp.float32)).astype(jnp.bfloat16)
            sums = sums + jnp.dot(high, value, preferred_element_type=jnp.float32)
            sums = sums + jnp.dot(low, value, preferred_element_type=jnp.float32)
        result = (sums / totals).astype(jnp.bfloat16)
        for place in range(group):
            out_ref[:total, place * HD : (place + 1) * HD] = result[place * total : (place + 1) * total]
        out_ref[total:, :] = jnp.zeros((rows, group * HD), jnp.bfloat16)
        out_ref[total:, :HD] = numbers_ref[...]

    return pl.pallas_call(
        kernel,
        out_shape=jax.ShapeDtypeStruct((total + rows, group * HD), jnp.bfloat16),
        in_specs=[whole()] * (2 + len(shifts) + len(passage_parts)),
        out_specs=whole(),
        scratch_shapes=[pltpu.VMEM((total, (group + 2) * HD), jnp.bfloat16)],
        compiler_params=params(6 * MIB),
        cost_estimate=staged(),
        name="attend",
    )(tile, *[arrived[shift] for shift in shifts], *passage_parts, ids)


def out_project(attention, weight, parts):
    width = attention[0].shape[1]
    rows = parts[0].shape[0]
    ctx_count = len(parts)
    total = rows * ctx_count
    columns = weight.shape[1]

    def kernel(*refs):
        attention_refs, weight_ref = refs[:ctx_count], refs[ctx_count]
        part_refs, (out_ref, raw_ref) = refs[ctx_count + 1 : -2], refs[-2:]
        here = lax.axis_index("ctx")
        for k in range(ctx_count):
            raw_ref[aligned(here ^ k, rows), :] = part_refs[k][:, aligned(here, columns)].astype(jnp.float32)
        product = jnp.zeros((total, columns), jnp.float32)
        for k in range(ctx_count):
            product = product + jnp.dot(
                attention_refs[k][:total, :],
                weight_ref[aligned(here ^ k, width), :],
                preferred_element_type=jnp.float32,
            )
        product = product.astype(jnp.bfloat16).astype(jnp.float32)
        out_ref[...] = (raw_ref[...] + product).astype(jnp.bfloat16)

    return pl.pallas_call(
        kernel,
        out_shape=jax.ShapeDtypeStruct((total, columns), jnp.bfloat16),
        in_specs=[whole()] * (2 * ctx_count + 1),
        out_specs=whole(),
        scratch_shapes=[pltpu.VMEM((total, columns), jnp.float32)],
        compiler_params=params(4 * MIB),
        cost_estimate=cost(flops=STAGE_FLOPS, bytes_accessed=2 * width * ctx_count * columns),
        name="out_project",
    )(*attention, kept(weight), *parts)


def route(mixed, gain, router, id_parts, slots):
    total, columns = mixed[0].shape
    ctx_count = len(mixed)
    rows = total // ctx_count
    width = columns * ctx_count
    expert_count = router.shape[0]

    def kernel(*refs):
        mixed_refs = refs[:ctx_count]
        gain_ref, router_ref = refs[ctx_count : ctx_count + 2]
        id_refs = refs[ctx_count + 2 : 2 * ctx_count + 2]
        own_ref, other_ref, rows_ref, place_ref, full_ref, ids_ref = refs[2 * ctx_count + 2 :]
        here = lax.axis_index("ctx")
        half = lax.axis_index("opt") // 2
        for k in range(ctx_count):
            full_ref[:, aligned(here ^ k, columns)] = mixed_refs[k][...].astype(jnp.float32)
            ids_ref[aligned(here ^ k, rows), :] = id_refs[k][total:, :HD].astype(jnp.float32)
        floats = full_ref[...]
        factor = lax.rsqrt(jnp.mean(floats * floats, axis=-1, keepdims=True) + EPS)
        expert_in = (floats * factor * gain_ref[...]).astype(jnp.bfloat16)
        rows_ref[...] = full_ref[aligned(here, rows), :].astype(jnp.bfloat16)
        logits = lax.dot_general(
            expert_in, router_ref[...], (((1,), (1,)), ((), ())), preferred_element_type=jnp.float32
        )
        ids = ids_ref[...].astype(jnp.int32)
        lane = lax.broadcasted_iota(jnp.int32, (total, expert_count), 1)
        first, second = lane == ids[:, 0:1], lane == ids[:, 1:2]
        one = jnp.sum(jnp.where(first, logits, 0.0), axis=1, keepdims=True)
        two = jnp.sum(jnp.where(second, logits, 0.0), axis=1, keepdims=True)
        top = jnp.maximum(one, two)
        one, two = jnp.exp(one - top), jnp.exp(two - top)
        share = jnp.where(first, one / (one + two), 0.0) + jnp.where(second, two / (one + two), 0.0)
        named = jnp.where(first | second, 1.0, 0.0)
        row = lax.broadcasted_iota(jnp.int32, (total, total), 0)
        column = lax.broadcasted_iota(jnp.int32, (total, total), 1)
        earlier = jnp.where(column < row, 1.0, 0.0).astype(jnp.bfloat16)
        rank = jnp.dot(earlier, named.astype(jnp.bfloat16), preferred_element_type=jnp.float32)

        def of(expert, table):
            return jnp.sum(jnp.where(lane == expert, table, 0.0), axis=1, keepdims=True)

        slot = lax.broadcasted_iota(jnp.int32, (total, 2 * slots), 1)
        hits, weights = [], []
        for expert, low in ((here * 2 + half, 0), (here * 2 + 1 - half, slots)):
            place = of(expert, rank).astype(jnp.int32) + low
            inside = (slot >= low) & (slot < low + slots) & (of(expert, named) > 0.5)
            hit = jnp.where(inside & (place == slot), 1.0, 0.0)
            hits.append(hit)
            weights.append(hit * of(expert, share))
        hits = hits[0] + hits[1]
        place_ref[...] = weights[0] + weights[1]
        chosen = lax.dot_general(
            hits.astype(jnp.bfloat16),
            expert_in,
            (((0,), (0,)), ((), ())),
            preferred_element_type=jnp.float32,
        )
        own_ref[...] = chosen[:slots].astype(jnp.bfloat16)
        other_ref[...] = chosen[slots:].astype(jnp.bfloat16)

    return pl.pallas_call(
        kernel,
        out_shape=[
            jax.ShapeDtypeStruct((slots, width), jnp.bfloat16),
            jax.ShapeDtypeStruct((slots, width), jnp.bfloat16),
            jax.ShapeDtypeStruct((rows, width), jnp.bfloat16),
            jax.ShapeDtypeStruct((total, 2 * slots), jnp.float32),
        ],
        in_specs=[whole()] * (2 * ctx_count + 2),
        out_specs=[whole()] * 4,
        scratch_shapes=[
            pltpu.VMEM((total, width), jnp.float32),
            pltpu.VMEM((total, HD), jnp.float32),
        ],
        compiler_params=params(6 * MIB),
        cost_estimate=staged(),
        name="route",
    )(*mixed, gain[None], router, *id_parts)


def experts(blocks, gate, up, down, tile):
    slots, width = blocks[0].shape
    count = slots * len(blocks)
    units = gate.shape[1]
    up_slots = 2
    tall = max(count, 128)

    def kernel(*refs):
        block_refs, refs = refs[: len(blocks)], refs[len(blocks) :]
        gate_ref, up_ref, down_ref, own_ref, other_ref, send_ref = refs[:6]
        rows_ref, hidden_ref, total_ref, ups_ref, up_sems = refs[6:]
        ups = Tiles(up_ref, ups_ref, up_sems)
        ups.open()
        for k in range(tall // slots):
            rows_ref[k * slots : (k + 1) * slots, :] = block_refs[k % len(blocks)][...]

        def add_down(i):
            at = slice(i * tile, (i + 1) * tile)
            hidden = hidden_ref[i % 2]
            for start in range(0, width, 2 * tile):
                cut = slice(start, start + 2 * tile)
                c = jnp.dot(hidden, down_ref[at, cut], preferred_element_type=jnp.float32)[:count]
                total_ref[:, cut] = c if i == 0 else total_ref[:, cut] + c

        for i in range(ups.count):
            at = slice(i * tile, (i + 1) * tile)
            a = jnp.dot(rows_ref[...], gate_ref[:, at], preferred_element_type=jnp.float32)[:count]
            b = jnp.dot(rows_ref[...], ups.ready(i), preferred_element_type=jnp.float32)[:count]
            ups.start(i + ups.slots)
            if i > 0:
                add_down(i - 1)
            hidden = (a / (1.0 + jnp.exp(-a)) * b).astype(jnp.bfloat16)
            for k in range(tall // count):
                hidden_ref[i % 2, k * count : (k + 1) * count, :] = hidden
        add_down(ups.count - 1)
        own_ref[...] = total_ref[:slots, :]
        other_ref[...] = total_ref[slots : 2 * slots, :]
        send_ref[...] = total_ref[2 * slots :, :].astype(jnp.bfloat16)

    return pl.pallas_call(
        kernel,
        out_shape=[
            pltpu.VMEM((slots, width), jnp.float32),
            pltpu.VMEM((slots, width), jnp.float32),
            pltpu.VMEM((2 * slots, width), jnp.bfloat16),
        ],
        in_specs=[whole()] * (len(blocks) + 1) + [anywhere(), whole()],
        out_specs=[whole()] * 3,
        scratch_shapes=[
            pltpu.VMEM((tall, width), jnp.bfloat16),
            pltpu.VMEM((2, tall, tile), jnp.bfloat16),
            pltpu.VMEM((count, width), jnp.float32),
            pltpu.VMEM((up_slots, width, tile), jnp.bfloat16),
            pltpu.SemaphoreType.DMA((up_slots,)),
        ],
        compiler_params=params(EXPERT_MIB * MIB),
        cost_estimate=cost(
            flops=6 * count * width * units, bytes_accessed=6 * width * units, transcendentals=count * units
        ),
        name="experts",
    )(*[kept(block) for block in blocks], kept(gate), up, kept(down))


def merge(other, from_core):
    slots, width = other.shape

    def kernel(mine_ref, core_ref, out_ref):
        out_ref[...] = (mine_ref[...] + core_ref[slots:, :].astype(jnp.float32)).astype(jnp.bfloat16)

    return pl.pallas_call(
        kernel,
        out_shape=jax.ShapeDtypeStruct((slots, width), jnp.bfloat16),
        in_specs=[whole()] * 2,
        out_specs=whole(),
        compiler_params=params(4 * MIB),
        name="merge",
    )(kept(other), from_core)


def combine(own, from_core, back, place, ctx_count):
    slots, width = back.shape
    total = place.shape[0]
    rows = total // ctx_count

    def kernel(mine_ref, core_ref, back_ref, place_ref, own_ref, *refs):
        send_refs, spread_ref = refs[:-1], refs[-1]
        here = lax.axis_index("ctx")
        own = mine_ref[...] + core_ref[:slots, :].astype(jnp.float32)
        both = jnp.concatenate([own, back_ref[...].astype(jnp.float32)], axis=0)
        spread_ref[...] = jnp.dot(
            place_ref[...], both, precision=lax.Precision.HIGHEST, preferred_element_type=jnp.float32
        )
        own_ref[...] = spread_ref[aligned(here, rows), :]
        for k, ref in enumerate(send_refs):
            ref[...] = spread_ref[aligned(here ^ (k + 1), rows), :].astype(jnp.bfloat16)

    out = pl.pallas_call(
        kernel,
        out_shape=[jax.ShapeDtypeStruct((rows, width), jnp.float32)]
        + [jax.ShapeDtypeStruct((rows, width), jnp.bfloat16)] * (ctx_count - 1),
        in_specs=[whole()] * 4,
        out_specs=[whole()] * ctx_count,
        scratch_shapes=[pltpu.VMEM((total, width), jnp.float32)],
        compiler_params=params(6 * MIB),
        name="combine",
    )(kept(own), from_core, back, place)
    return out[0], out[1:]


def fast_shards(*args):
    return fast_layer(*args)


def fast_layer(
    options,
    cache_keys,
    cache_values,
    attention_gain,
    expert_gain,
    input_weight,
    output_weight,
    router_weight,
    gate_weight,
    up_weight,
    down_weight,
    routing,
):
    own_rows = options[0]
    local_rows, _ = own_rows.shape
    ctx_count = lax.axis_size("ctx")
    option_len = local_rows * ctx_count
    passage_rows = cache_keys.shape[0]
    passage = passage_rows * ctx_count
    slots = MOST * ctx_count
    plan = head_plan(ctx_count, input_weight.shape[1] // HD)
    tile = 4 * HD

    parts = gathered(own_rows, "ctx")

    half_dim = HD // 2
    inverse = THETA ** (-2.0 * jnp.arange(half_dim, dtype=jnp.float32) / HD)
    positions = (passage + jnp.arange(option_len)).astype(jnp.float32)
    angles = positions[:, None] * inverse[None, :]
    cosine, sine = jnp.cos(angles), jnp.sin(angles)
    cosine = jnp.concatenate([cosine, cosine], axis=1)
    sine = jnp.concatenate([-sine, sine], axis=1)
    cosine, sine = tables(cosine, sine)

    packed = pack(cache_keys, cache_values, routing[0].T, cosine)
    opt_count = lax.axis_size("opt")
    places = [(c, o) for c in range(ctx_count) for o in range(opt_count)]
    to_one = [(c * opt_count + o, (c ^ (1 + o % 2)) * opt_count + o) for c, o in places]
    one = lax.ppermute(packed[1], ("ctx", "opt"), to_one)
    third = flip(packed[2], "ctx", 3)

    product, payloads = project(parts, attention_gain, input_weight, cosine, sine, plan)
    arrived = {shift: lax.ppermute(payloads[shift], "ctx", plan[2][shift]) for shift in HEADS_ORDER}
    passage_parts = [packed[0], one, flip(one, "opt", 1), third, flip(third, "opt", 1)]
    attention = attend(product, arrived, passage_parts, packed[3], plan)
    attention = gathered(attention, "ctx")
    mixed = out_project(attention, output_weight, parts)
    mixed = gathered(mixed, "ctx")
    own_slots, other_slots, mixed_rows, place = route(
        mixed, expert_gain, router_weight.T, attention, slots
    )
    from_x = flip(other_slots, "opt", 2)
    core_own = flip(own_slots, "opt", 1)
    core_x = flip(from_x, "opt", 1)
    own, other, send = experts(
        [own_slots, from_x, core_own, core_x], gate_weight, up_weight, down_weight, tile
    )
    from_core = flip(send, "opt", 1)
    back = flip(merge(other, from_core), "opt", 2)
    own_sum, sends = combine(own, from_core, back, place, ctx_count)
    total = mixed_rows.astype(jnp.float32) + own_sum
    for mask in range(ctx_count - 1, 0, -1):
        total = total + flip(sends[mask - 1], "ctx", mask).astype(jnp.float32)
    return total.astype(jnp.bfloat16)[None]


def takes_fast(mesh, input_weight, output_weight, router_weight, gate_weight):
    ctx_count, opt_count = mesh.shape["ctx"], mesh.shape["opt"]
    devices = ctx_count * opt_count
    return (
        ctx_count == KVH
        and opt_count == 4
        and router_weight.shape[1] == 2 * ctx_count
        and gate_weight.shape[1] == devices * (FF // 2)
        and input_weight.shape[1] % (ctx_count * HD) == 0
        and output_weight.shape[1] % (ctx_count * HD) == 0
    )


def solution(mesh):
    placed = (
        P(("parts", "opt"), "ctx", None),
        P(("parts", "ctx"), None),
        P(("parts", "ctx"), None),
        P(),
        P(),
        P(None, "ctx"),
        P(None, "ctx"),
        P(),
        P(None, ("ctx", "opt")),
        P(None, ("ctx", "opt")),
        P(("ctx", "opt"), None),
        P(("parts", "opt"), "ctx", None),
    )

    def layer(*args):
        fast = takes_fast(mesh, args[5], args[6], args[7], args[8])
        return jax.shard_map(
            fast_shards if fast else general_shards,
            mesh=mesh,
            in_specs=placed,
            out_specs=P(("parts", "opt"), "ctx", None),
            check_vma=False,
        )(*args)

    return layer
```

profile of v0, /device:TPU:0, one launch (start us, length us, event | category | flops | bytes accessed | tf_op | source)
XLA Modules:
  0.0 74.8 jit_solution(18320738821021437903)
XLA Ops:
  0.0 0.1 fusion.1
  0.2 0.1 pad_maximum_fusion
  0.3 0.0 copy-start.1
  0.3 0.4 copy-done.6
  0.7 0.2 copy-done.3
  0.9 0.1 copy-done.2
  1.0 0.1 pack.1
  1.1 3.1 %collective-permute-start.6 = (bf16[128,256]{1,0:T(8,128)(2,1)S(1)}, bf16[128,256]{1,0:T(8,128)(2,1)S(1)}, u32[]{:S(2)}, u32[]{:S(2)}) collective-permute-start(bf16[128,256]{1,0:T(8,128)(2,1)S(1)} %get-tuple-element.33), channel_id=1, source_target_pairs={{0,4},{1,9},{2,6},{3,11},{4,0},{5,13},{6,2},{7,15},{8,12},{9,1},{1... | collective-permute-start | bytes 196616 | tf_op jit(solution)/shard_map/ppermute | solution.py:760
  4.2 2.5 %collective-permute-start.2 = (bf16[8,3072]{1,0:T(8,128)(2,1)S(1)}, bf16[8,3072]{1,0:T(8,128)(2,1)S(1)}, u32[]{:S(2)}, u32[]{:S(2)}) collective-permute-start(bf16[8,3072]{1,0:T(8,128)(2,1)S(1)} %bitcast.15), channel_id=1, source_target_pairs={{0,12},{4,8},{8,4},{12,0},{1,13},{5,9},{9,5},{13,1},{2,14},{6,10},... | collective-permute-start | bytes 147464 | tf_op jit(solution)/shard_map/ppermute | solution.py:236
  6.6 0.1 collective-permute-start.1
  6.8 1.8 %collective-permute-start = (bf16[8,3072]{1,0:T(8,128)(2,1)S(1)}, bf16[8,3072]{1,0:T(8,128)(2,1)S(1)}, u32[]{:S(2)}, u32[]{:S(2)}) collective-permute-start(bf16[8,3072]{1,0:T(8,128)(2,1)S(1)} %bitcast.17), channel_id=1, source_target_pairs={{0,4},{4,0},{8,12},{12,8},{1,5},{5,1},{9,13},{13,9},{2,6},{6,2},{1... | collective-permute-start | bytes 147464 | tf_op jit(solution)/shard_map/ppermute | solution.py:236
  8.6 2.5 %collective-permute-start.8 = (bf16[64,256]{1,0:T(8,128)(2,1)S(1)}, bf16[64,256]{1,0:T(8,128)(2,1)S(1)}, u32[]{:S(2)}, u32[]{:S(2)}) collective-permute-start(bf16[64,256]{1,0:T(8,128)(2,1)S(1)} %get-tuple-element.34), channel_id=1, source_target_pairs={{0,12},{4,8},{8,4},{12,0},{1,13},{5,9},{9,5},{13,1},{2,14},{6,10},... | collective-permute-start | bytes 98312 | tf_op jit(solution)/shard_map/ppermute | solution.py:236
  11.0 0.0 collective-permute-start.7
  11.0 0.0 collective-permute-done.2.refs_3_.refs_8_
  11.0 1.6 %collective-permute-done.1.refs_2_.refs_7_ = bf16[8,3072]{1,0:T(8,128)(2,1)S(1)} collective-permute-done((bf16[8,3072]{1,0:T(8,128)(2,1)S(1)}, bf16[8,3072]{1,0:T(8,128)(2,1)S(1)}, u32[]{:S(2)}, u32[]{:S(2)}) %collective-permute-start.1) | collective-permute-done | bytes 49184 | tf_op jit(solution)/shard_map/ppermute | solution.py:236
  12.7 1.4 %project.1 = (bf16[32,1024]{1,0:T(8,128)(2,1)S(1)}, bf16[32,768]{1,0:T(8,128)(2,1)S(1)}, bf16[32,256]{1,0:T(8,128)(2,1)S(1)}, bf16[32,256]{1,0:T(8,128)(2,1)S(1)}) custom-call(bf16[8,3072]{1,0:T(8,128)(2,1)S(1)} %bitcast.18, bf16[8,3072]{1,0:T(8,128)(2,1)S(1)} %collective-permute-done.refs_1_.refs_6_, ...), custom_call_target="tpu_custom_call" | custom-call | bytes 6291456 | tf_op jit(solution)/shard_map/project/pallas_call | solution.py:406
  14.1 0.5 collective-permute-start.3
  14.6 0.0 collective-permute-done.8.refs_7_
  14.6 0.0 collective-permute-start.9
  14.6 0.7 collective-permute-start.4
  15.3 0.7 collective-permute-start.5
  16.0 0.0 collective-permute-done.4.refs_2_
  16.0 0.0 collective-permute-done.5.refs_3_
  16.0 4.1 %collective-permute-done.3.refs_1_ = bf16[32,768]{1,0:T(8,128)(2,1)S(1)} collective-permute-done((bf16[32,768]{1,0:T(8,128)(2,1)S(1)}, bf16[32,768]{1,0:T(8,128)(2,1)S(1)}, u32[]{:S(2)}, u32[]{:S(2)}) %collective-permute-start.3) | collective-permute-done | bytes 49184 | tf_op jit(solution)/shard_map/ppermute | solution.py:764
  20.1 0.0 slice-start.6
  20.1 0.0 slice-start.7
  20.1 0.9 %attend.1.refs_0_.refs_6_ = bf16[40,768]{1,0:T(8,128)(2,1)S(1)} custom-call(bf16[32,1024]{1,0:T(8,128)(2,1)S(1)} %get-tuple-element.28.refs_0_, bf16[32,768]{1,0:T(8,128)(2,1)S(1)} %collective-permute-done.3.refs_1_, bf16[32,256]{1,0:T(8,128)(2,1)S(1)} %collective-permute-done.4.refs_2_, bf16[32,256]{1,0:T(8,128)(2,1)S(1)} %collective-permute-done.5.refs_3_, ...), custom_call_target="tpu_custom_call" | custom-call | flops 8000000000 | tf_op jit(solution)/shard_map/attend/pallas_call | solution.py:481
  21.0 0.0 slice-start
  21.0 0.0 slice-start.1
  21.0 0.0 slice-start.2
  21.0 0.0 slice-start.8
  21.0 0.0 slice-start.9
  21.0 3.1 %collective-permute-start.12 = (bf16[40,768]{1,0:T(8,128)(2,1)S(1)}, bf16[40,768]{1,0:T(8,128)(2,1)S(1)}, u32[]{:S(2)}, u32[]{:S(2)}) collective-permute-start(bf16[40,768]{1,0:T(8,128)(2,1)S(1)} %attend.1.refs_0_.refs_6_), channel_id=1, source_target_pairs={{0,12},{4,8},{8,4},{12,0},{1,13},{5,9},{9,5},{13,1},{2,14},{6,10},... | collective-permute-start | bytes 184328 | tf_op jit(solution)/shard_map/ppermute | solution.py:236
  24.1 1.0 %collective-permute-start.11 = (bf16[40,768]{1,0:T(8,128)(2,1)S(1)}, bf16[40,768]{1,0:T(8,128)(2,1)S(1)}, u32[]{:S(2)}, u32[]{:S(2)}) collective-permute-start(bf16[40,768]{1,0:T(8,128)(2,1)S(1)} %attend.1.refs_0_.refs_6_), channel_id=1, source_target_pairs={{0,8},{4,12},{8,0},{12,4},{1,9},{5,13},{9,1},{13,5},{2,10},{6,14},... | collective-permute-start | bytes 184328 | tf_op jit(solution)/shard_map/ppermute | solution.py:236
  25.1 0.4 collective-permute-start.10
  25.5 1.7 %collective-permute-done.12.refs_3_.refs_9_ = bf16[40,768]{1,0:T(8,128)(2,1)S(1)} collective-permute-done((bf16[40,768]{1,0:T(8,128)(2,1)S(1)}, bf16[40,768]{1,0:T(8,128)(2,1)S(1)}, u32[]{:S(2)}, u32[]{:S(2)}) %collective-permute-start.12) | collective-permute-done | bytes 61472 | tf_op jit(solution)/shard_map/ppermute | solution.py:236
  27.2 3.2 %collective-permute-done.11.refs_2_.refs_8_ = bf16[40,768]{1,0:T(8,128)(2,1)S(1)} collective-permute-done((bf16[40,768]{1,0:T(8,128)(2,1)S(1)}, bf16[40,768]{1,0:T(8,128)(2,1)S(1)}, u32[]{:S(2)}, u32[]{:S(2)}) %collective-permute-start.11) | collective-permute-done | bytes 61472 | tf_op jit(solution)/shard_map/ppermute | solution.py:236
  30.4 0.0 collective-permute-done.10.refs_1_.refs_7_
  30.4 0.9 %out_project.1.refs_0_ = bf16[32,768]{1,0:T(8,128)(2,1)S(1)} custom-call(bf16[40,768]{1,0:T(8,128)(2,1)S(1)} %attend.1.refs_0_.refs_6_, bf16[40,768]{1,0:T(8,128)(2,1)S(1)} %collective-permute-done.10.refs_1_.refs_7_, bf16[40,768]{1,0:T(8,128)(2,1)S(1)} %collective-permute-done.11.refs_2_.refs_8_, ...), custom_call_target="tpu_custom_call" | custom-call | flops 8000000000 | bytes 4718592 | tf_op jit(solution)/shard_map/out_project/pallas_call | solution.py:516
  31.4 2.9 %collective-permute-start.15 = (bf16[32,768]{1,0:T(8,128)(2,1)S(1)}, bf16[32,768]{1,0:T(8,128)(2,1)S(1)}, u32[]{:S(2)}, u32[]{:S(2)}) collective-permute-start(bf16[32,768]{1,0:T(8,128)(2,1)S(1)} %out_project.1.refs_0_), channel_id=1, source_target_pairs={{0,12},{4,8},{8,4},{12,0},{1,13},{5,9},{9,5},{13,1},{2,14},{6,10},... | collective-permute-start | bytes 147464 | tf_op jit(solution)/shard_map/ppermute | solution.py:236
  34.3 0.0 collective-permute-start.14
  34.3 1.5 %collective-permute-start.13 = (bf16[32,768]{1,0:T(8,128)(2,1)S(1)}, bf16[32,768]{1,0:T(8,128)(2,1)S(1)}, u32[]{:S(2)}, u32[]{:S(2)}) collective-permute-start(bf16[32,768]{1,0:T(8,128)(2,1)S(1)} %out_project.1.refs_0_), channel_id=1, source_target_pairs={{0,4},{4,0},{8,12},{12,8},{1,5},{5,1},{9,13},{13,9},{2,6},{6,2},{1... | collective-permute-start | bytes 147464 | tf_op jit(solution)/shard_map/ppermute | solution.py:236
  35.8 1.5 %collective-permute-done.15.refs_3_ = bf16[32,768]{1,0:T(8,128)(2,1)S(1)} collective-permute-done((bf16[32,768]{1,0:T(8,128)(2,1)S(1)}, bf16[32,768]{1,0:T(8,128)(2,1)S(1)}, u32[]{:S(2)}, u32[]{:S(2)}) %collective-permute-start.15) | collective-permute-done | bytes 49184 | tf_op jit(solution)/shard_map/ppermute | solution.py:236
  37.4 1.9 %collective-permute-done.14.refs_2_ = bf16[32,768]{1,0:T(8,128)(2,1)S(1)} collective-permute-done((bf16[32,768]{1,0:T(8,128)(2,1)S(1)}, bf16[32,768]{1,0:T(8,128)(2,1)S(1)}, u32[]{:S(2)}, u32[]{:S(2)}) %collective-permute-start.14) | collective-permute-done | bytes 49184 | tf_op jit(solution)/shard_map/ppermute | solution.py:236
  39.3 0.1 collective-permute-done.13.refs_1_
  39.4 0.0 slice-start.5
  39.4 0.0 slice-start.10
  39.4 0.6 route.1
  40.0 1.6 %collective-permute-start.16 = (bf16[16,3072]{1,0:T(8,128)(2,1)S(1)}, bf16[16,3072]{1,0:T(8,128)(2,1)S(1)}, u32[]{:S(2)}, u32[]{:S(2)}) collective-permute-start(bf16[16,3072]{1,0:T(8,128)(2,1)S(1)} %get-tuple-element.38), channel_id=1, source_target_pairs={{0,2},{1,3},{2,0},{3,1},{4,6},{5,7},{6,4},{7,5},{8,10},{9,11},{10,... | collective-permute-start | bytes 294920 | tf_op jit(solution)/shard_map/ppermute | solution.py:236
  41.6 3.1 %collective-permute-done.16.refs_1_ = bf16[16,3072]{1,0:T(8,128)(2,1)S(1)} collective-permute-done((bf16[16,3072]{1,0:T(8,128)(2,1)S(1)}, bf16[16,3072]{1,0:T(8,128)(2,1)S(1)}, u32[]{:S(2)}, u32[]{:S(2)}) %collective-permute-start.16) | collective-permute-done | bytes 98336 | tf_op jit(solution)/shard_map/ppermute | solution.py:236
  44.7 1.3 %collective-permute-done.18.refs_3_ = bf16[16,3072]{1,0:T(8,128)(2,1)S(1)} collective-permute-done((bf16[16,3072]{1,0:T(8,128)(2,1)S(1)}, bf16[16,3072]{1,0:T(8,128)(2,1)S(1)}, u32[]{:S(2)}, u32[]{:S(2)}) %collective-permute-start.18) | collective-permute-done | bytes 98336 | tf_op jit(solution)/shard_map/ppermute | solution.py:236
  46.1 0.3 slice-done.11
  46.4 13.2 %experts.1 = (f32[16,3072]{1,0:T(8,128)S(1)}, f32[16,3072]{1,0:T(8,128)S(1)}, bf16[32,3072]{1,0:T(8,128)(2,1)S(1)}) custom-call(bf16[16,3072]{1,0:T(8,128)(2,1)S(1)} %get-tuple-element.37.refs_0_, bf16[16,3072]{1,0:T(8,128)(2,1)S(1)} %collective-permute-done.16.refs_1_, bf16[16,3072]{1,0:T(8,128)(2,1)S(1)} %collective-permute-done.17.refs_2_, ...), custom_call_target="tpu_custom_call" | custom-call | flops 4831838208 | bytes 75497472 | tf_op jit(solution)/shard_map/experts/pallas_call | solution.py:647
  59.7 0.1 collective-permute-start.19
  59.8 1.4 %collective-permute-done.19.core_ref = bf16[32,3072]{1,0:T(8,128)(2,1)S(1)} collective-permute-done((bf16[32,3072]{1,0:T(8,128)(2,1)S(1)}, bf16[32,3072]{1,0:T(8,128)(2,1)S(1)}, u32[]{:S(2)}, u32[]{:S(2)}) %collective-permute-start.19) | collective-permute-done | bytes 196640 | tf_op jit(solution)/shard_map/ppermute | solution.py:236
  61.2 1.6 %collective-permute-start.20 = (bf16[16,3072]{1,0:T(8,128)(2,1)S(1)}, bf16[16,3072]{1,0:T(8,128)(2,1)S(1)}, u32[]{:S(2)}, u32[]{:S(2)}) collective-permute-start(bf16[16,3072]{1,0:T(8,128)(2,1)S(1)} %merge.1), channel_id=1, source_target_pairs={{0,2},{1,3},{2,0},{3,1},{4,6},{5,7},{6,4},{7,5},{8,10},{9,11},{10,... | collective-permute-start | bytes 294920 | tf_op jit(solution)/shard_map/ppermute | solution.py:236
  62.8 3.3 %collective-permute-done.20.back_ref = bf16[16,3072]{1,0:T(8,128)(2,1)S(1)} collective-permute-done((bf16[16,3072]{1,0:T(8,128)(2,1)S(1)}, bf16[16,3072]{1,0:T(8,128)(2,1)S(1)}, u32[]{:S(2)}, u32[]{:S(2)}) %collective-permute-start.20) | collective-permute-done | bytes 98336 | tf_op jit(solution)/shard_map/ppermute | solution.py:236
  66.1 0.5 combine.1
  66.6 2.0 %collective-permute-start.21 = (bf16[8,3072]{1,0:T(8,128)(2,1)S(1)}, bf16[8,3072]{1,0:T(8,128)(2,1)S(1)}, u32[]{:S(2)}, u32[]{:S(2)}) collective-permute-start(bf16[8,3072]{1,0:T(8,128)(2,1)S(1)} %get-tuple-element.44), channel_id=1, source_target_pairs={{0,12},{4,8},{8,4},{12,0},{1,13},{5,9},{9,5},{13,1},{2,14},{6,10},... | collective-permute-start | bytes 147464 | tf_op jit(solution)/shard_map/ppermute | solution.py:236
  68.6 0.1 collective-permute-start.22
  68.7 2.4 %collective-permute-start.23 = (bf16[8,3072]{1,0:T(8,128)(2,1)S(1)}, bf16[8,3072]{1,0:T(8,128)(2,1)S(1)}, u32[]{:S(2)}, u32[]{:S(2)}) collective-permute-start(bf16[8,3072]{1,0:T(8,128)(2,1)S(1)} %get-tuple-element.46), channel_id=1, source_target_pairs={{0,4},{4,0},{8,12},{12,8},{1,5},{5,1},{9,13},{13,9},{2,6},{6,2},{1... | collective-permute-start | bytes 147464 | tf_op jit(solution)/shard_map/ppermute | solution.py:236
  71.0 1.8 %collective-permute-done.21 = bf16[8,3072]{1,0:T(8,128)(2,1)S(1)} collective-permute-done((bf16[8,3072]{1,0:T(8,128)(2,1)S(1)}, bf16[8,3072]{1,0:T(8,128)(2,1)S(1)}, u32[]{:S(2)}, u32[]{:S(2)}) %collective-permute-start.21) | collective-permute-done | bytes 49184 | tf_op jit(solution)/shard_map/ppermute | solution.py:236
  72.8 1.3 %collective-permute-done.22 = bf16[8,3072]{1,0:T(8,128)(2,1)S(1)} collective-permute-done((bf16[8,3072]{1,0:T(8,128)(2,1)S(1)}, bf16[8,3072]{1,0:T(8,128)(2,1)S(1)}, u32[]{:S(2)}, u32[]{:S(2)}) %collective-permute-start.22) | collective-permute-done | bytes 49184 | tf_op jit(solution)/shard_map/ppermute | solution.py:236
  74.1 0.7 fusion
  (48 shorter events, 0.1 us)
Async XLA Ops:
  0.0 0.7 copy-start.6
  0.0 0.9 %copy-start.3 = (bf16[128,512]{1,0:T(8,128)(2,1)S(1)}, bf16[128,512]{1,0:T(8,128)(2,1)}, u32[]{:S(2)}) copy-start(bf16[128,512]{1,0:T(8,128)(2,1)} %values_ref.1) | copy-start | bytes 393220
  0.0 1.0 %copy-start.2 = (bf16[128,512]{1,0:T(8,128)(2,1)S(1)}, bf16[128,512]{1,0:T(8,128)(2,1)}, u32[]{:S(2)}) copy-start(bf16[128,512]{1,0:T(8,128)(2,1)} %keys_ref.1) | copy-start | bytes 393220
  0.3 3.9 %copy-start = (bf16[1,8,3072]{2,1,0:T(8,128)(2,1)S(1)}, bf16[1,8,3072]{2,1,0:T(8,128)(2,1)}, u32[]{:S(2)}) copy-start(bf16[1,8,3072]{2,1,0:T(8,128)(2,1)} %param.12) | copy-start | bytes 147460
  0.3 12.4 %slice-start.12 = ((s8[6291456]{0:T(1024)(128)(4,1)}), s8[4194304]{0:T(1024)(128)(4,1)S(1)}, s32[]{:S(2)}) async-start(s8[6291456]{0:T(1024)(128)(4,1)} %bitcast.13), calls=%async_computation.12 | async-start | bytes 8388608
  0.3 12.4 %copy-start.1 = (f32[3072]{0:T(1024)S(1)}, f32[3072]{0:T(1024)}, u32[]{:S(2)}) copy-start(f32[3072]{0:T(1024)} %param.15) | copy-start | bytes 36868
  1.0 11.7 %slice-start.13 = ((s8[6291456]{0:T(1024)(128)(4,1)}), s8[2097152]{0:T(1024)(128)(4,1)S(1)}, s32[]{:S(2)}) async-start(s8[6291456]{0:T(1024)(128)(4,1)} %bitcast.13), calls=%async_computation.13 | async-start | bytes 4194304
  1.1 29.4 %slice-start.14 = ((s8[4718592]{0:T(1024)(128)(4,1)}), s8[4194304]{0:T(1024)(128)(4,1)S(1)}, s32[]{:S(2)}) async-start(s8[4718592]{0:T(1024)(128)(4,1)} %bitcast.21), calls=%async_computation.14 | async-start | bytes 8388608
  1.1 10.0 %collective-permute-start.6 = (bf16[128,256]{1,0:T(8,128)(2,1)S(1)}, bf16[128,256]{1,0:T(8,128)(2,1)S(1)}, u32[]{:S(2)}, u32[]{:S(2)}) collective-permute-start(bf16[128,256]{1,0:T(8,128)(2,1)S(1)} %get-tuple-element.33), channel_id=1, source_target_pairs={{0,4},{1,9},{2,6},{3,11},{4,0},{5,13},{6,2},{7,15},{8,12},{9,1},{1... | collective-permute-start | bytes 196616 | tf_op jit(solution)/shard_map/ppermute | solution.py:760
  4.2 6.9 %collective-permute-start.2 = (bf16[8,3072]{1,0:T(8,128)(2,1)S(1)}, bf16[8,3072]{1,0:T(8,128)(2,1)S(1)}, u32[]{:S(2)}, u32[]{:S(2)}) collective-permute-start(bf16[8,3072]{1,0:T(8,128)(2,1)S(1)} %bitcast.15), channel_id=1, source_target_pairs={{0,12},{4,8},{8,4},{12,0},{1,13},{5,9},{9,5},{13,1},{2,14},{6,10},... | collective-permute-start | bytes 147464 | tf_op jit(solution)/shard_map/ppermute | solution.py:236
  6.6 6.0 %collective-permute-start.1 = (bf16[8,3072]{1,0:T(8,128)(2,1)S(1)}, bf16[8,3072]{1,0:T(8,128)(2,1)S(1)}, u32[]{:S(2)}, u32[]{:S(2)}) collective-permute-start(bf16[8,3072]{1,0:T(8,128)(2,1)S(1)} %bitcast.16), channel_id=1, source_target_pairs={{0,8},{4,12},{8,0},{12,4},{1,9},{5,13},{9,1},{13,5},{2,10},{6,14},... | collective-permute-start | bytes 147464 | tf_op jit(solution)/shard_map/ppermute | solution.py:236
  6.8 5.9 %collective-permute-start = (bf16[8,3072]{1,0:T(8,128)(2,1)S(1)}, bf16[8,3072]{1,0:T(8,128)(2,1)S(1)}, u32[]{:S(2)}, u32[]{:S(2)}) collective-permute-start(bf16[8,3072]{1,0:T(8,128)(2,1)S(1)} %bitcast.17), channel_id=1, source_target_pairs={{0,4},{4,0},{8,12},{12,8},{1,5},{5,1},{9,13},{13,9},{2,6},{6,2},{1... | collective-permute-start | bytes 147464 | tf_op jit(solution)/shard_map/ppermute | solution.py:236
  8.6 6.1 %collective-permute-start.8 = (bf16[64,256]{1,0:T(8,128)(2,1)S(1)}, bf16[64,256]{1,0:T(8,128)(2,1)S(1)}, u32[]{:S(2)}, u32[]{:S(2)}) collective-permute-start(bf16[64,256]{1,0:T(8,128)(2,1)S(1)} %get-tuple-element.34), channel_id=1, source_target_pairs={{0,12},{4,8},{8,4},{12,0},{1,13},{5,9},{9,5},{13,1},{2,14},{6,10},... | collective-permute-start | bytes 98312 | tf_op jit(solution)/shard_map/ppermute | solution.py:236
  11.0 9.1 %collective-permute-start.7 = (bf16[128,256]{1,0:T(8,128)(2,1)S(1)}, bf16[128,256]{1,0:T(8,128)(2,1)S(1)}, u32[]{:S(2)}, u32[]{:S(2)}) collective-permute-start(bf16[128,256]{1,0:T(8,128)(2,1)S(1)} %collective-permute-done.6.refs_5_), channel_id=1, source_target_pairs={{0,1},{1,0},{2,3},{3,2},{4,5},{5,4},{6,7},{7,6},{8,9},{9,8},{10,11... | collective-permute-start | bytes 196616 | tf_op jit(solution)/shard_map/ppermute | solution.py:236
  14.1 5.9 %collective-permute-start.3 = (bf16[32,768]{1,0:T(8,128)(2,1)S(1)}, bf16[32,768]{1,0:T(8,128)(2,1)S(1)}, u32[]{:S(2)}, u32[]{:S(2)}) collective-permute-start(bf16[32,768]{1,0:T(8,128)(2,1)S(1)} %get-tuple-element.29), channel_id=1, source_target_pairs={{0,4},{4,8},{8,12},{12,0},{1,5},{5,9},{9,13},{13,1},{2,6},{6,10},{... | collective-permute-start | bytes 147464 | tf_op jit(solution)/shard_map/ppermute | solution.py:764
  14.6 1.4 %collective-permute-start.9 = (bf16[64,256]{1,0:T(8,128)(2,1)S(1)}, bf16[64,256]{1,0:T(8,128)(2,1)S(1)}, u32[]{:S(2)}, u32[]{:S(2)}) collective-permute-start(bf16[64,256]{1,0:T(8,128)(2,1)S(1)} %collective-permute-done.8.refs_7_), channel_id=1, source_target_pairs={{0,1},{1,0},{2,3},{3,2},{4,5},{5,4},{6,7},{7,6},{8,9},{9,8},{10,11... | collective-permute-start | bytes 98312 | tf_op jit(solution)/shard_map/ppermute | solution.py:236
  14.6 1.3 %collective-permute-start.4 = (bf16[32,256]{1,0:T(8,128)(2,1)S(1)}, bf16[32,256]{1,0:T(8,128)(2,1)S(1)}, u32[]{:S(2)}, u32[]{:S(2)}) collective-permute-start(bf16[32,256]{1,0:T(8,128)(2,1)S(1)} %get-tuple-element.30), channel_id=1, source_target_pairs={{12,4},{13,5},{14,6},{15,7},{28,20},{29,21},{30,22},{31,23}} | collective-permute-start | bytes 49160 | tf_op jit(solution)/shard_map/ppermute | solution.py:764
  15.3 0.7 collective-permute-start.5
  20.1 10.3 %slice-start.15 = ((s8[4718592]{0:T(1024)(128)(4,1)}), s8[524288]{0:T(1024)(128)(4,1)S(1)}, s32[]{:S(2)}) async-start(s8[4718592]{0:T(1024)(128)(4,1)} %bitcast.21), calls=%async_computation.15 | async-start | bytes 1048576
  20.1 19.3 %copy-start.4 = (bf16[3072,8]{0,1:T(8,128)(2,1)S(1)}, bf16[3072,8]{0,1:T(8,128)(2,1)}, u32[]{:S(2)}) copy-start(bf16[3072,8]{0,1:T(8,128)(2,1)} %param.19) | copy-start | bytes 147460
  20.1 19.3 %copy-start.5 = (f32[3072]{0:T(1024)S(1)}, f32[3072]{0:T(1024)}, u32[]{:S(2)}) copy-start(f32[3072]{0:T(1024)} %param.16) | copy-start | bytes 36868
  20.1 25.9 %slice-start.6 = ((s8[25165824]{0:T(1024)(128)(4,1)}), s8[4194304]{0:T(1024)(128)(4,1)S(1)}, s32[]{:S(2)}) async-start(s8[25165824]{0:T(1024)(128)(4,1)} %bitcast.11), calls=%async_computation.6 | async-start | bytes 8388608
  20.1 25.9 %slice-start.7 = ((s8[25165824]{0:T(1024)(128)(4,1)}), s8[4194304]{0:T(1024)(128)(4,1)S(1)}, s32[]{:S(2)}) async-start(s8[25165824]{0:T(1024)(128)(4,1)} %bitcast.11), calls=%async_computation.7 | async-start | bytes 8388608
  21.0 25.0 %slice-start = ((s8[25165824]{0:T(1024)(128)(4,1)}), s8[4194304]{0:T(1024)(128)(4,1)S(1)}, s32[]{:S(2)}) async-start(s8[25165824]{0:T(1024)(128)(4,1)} %bitcast.9), calls=%async_computation | async-start | bytes 8388608
  21.0 25.0 %slice-start.1 = ((s8[25165824]{0:T(1024)(128)(4,1)}), s8[4194304]{0:T(1024)(128)(4,1)S(1)}, s32[]{:S(2)}) async-start(s8[25165824]{0:T(1024)(128)(4,1)} %bitcast.9), calls=%async_computation.1 | async-start | bytes 8388608
  21.0 25.0 %slice-start.2 = ((s8[25165824]{0:T(1024)(128)(4,1)}), s8[4194304]{0:T(1024)(128)(4,1)S(1)}, s32[]{:S(2)}) async-start(s8[25165824]{0:T(1024)(128)(4,1)} %bitcast.9), calls=%async_computation.2 | async-start | bytes 8388608
  21.0 25.0 %slice-start.8 = ((s8[25165824]{0:T(1024)(128)(4,1)}), s8[4194304]{0:T(1024)(128)(4,1)S(1)}, s32[]{:S(2)}) async-start(s8[25165824]{0:T(1024)(128)(4,1)} %bitcast.11), calls=%async_computation.8 | async-start | bytes 8388608
  21.0 25.0 %slice-start.9 = ((s8[25165824]{0:T(1024)(128)(4,1)}), s8[4194304]{0:T(1024)(128)(4,1)S(1)}, s32[]{:S(2)}) async-start(s8[25165824]{0:T(1024)(128)(4,1)} %bitcast.11), calls=%async_computation.9 | async-start | bytes 8388608
  21.0 6.1 %collective-permute-start.12 = (bf16[40,768]{1,0:T(8,128)(2,1)S(1)}, bf16[40,768]{1,0:T(8,128)(2,1)S(1)}, u32[]{:S(2)}, u32[]{:S(2)}) collective-permute-start(bf16[40,768]{1,0:T(8,128)(2,1)S(1)} %attend.1.refs_0_.refs_6_), channel_id=1, source_target_pairs={{0,12},{4,8},{8,4},{12,0},{1,13},{5,9},{9,5},{13,1},{2,14},{6,10},... | collective-permute-start | bytes 184328 | tf_op jit(solution)/shard_map/ppermute | solution.py:236
  24.1 6.3 %collective-permute-start.11 = (bf16[40,768]{1,0:T(8,128)(2,1)S(1)}, bf16[40,768]{1,0:T(8,128)(2,1)S(1)}, u32[]{:S(2)}, u32[]{:S(2)}) collective-permute-start(bf16[40,768]{1,0:T(8,128)(2,1)S(1)} %attend.1.refs_0_.refs_6_), channel_id=1, source_target_pairs={{0,8},{4,12},{8,0},{12,4},{1,9},{5,13},{9,1},{13,5},{2,10},{6,14},... | collective-permute-start | bytes 184328 | tf_op jit(solution)/shard_map/ppermute | solution.py:236
  25.1 5.3 %collective-permute-start.10 = (bf16[40,768]{1,0:T(8,128)(2,1)S(1)}, bf16[40,768]{1,0:T(8,128)(2,1)S(1)}, u32[]{:S(2)}, u32[]{:S(2)}) collective-permute-start(bf16[40,768]{1,0:T(8,128)(2,1)S(1)} %attend.1.refs_0_.refs_6_), channel_id=1, source_target_pairs={{0,4},{4,0},{8,12},{12,8},{1,5},{5,1},{9,13},{13,9},{2,6},{6,2},{1... | collective-permute-start | bytes 184328 | tf_op jit(solution)/shard_map/ppermute | solution.py:236
  31.4 6.0 %collective-permute-start.15 = (bf16[32,768]{1,0:T(8,128)(2,1)S(1)}, bf16[32,768]{1,0:T(8,128)(2,1)S(1)}, u32[]{:S(2)}, u32[]{:S(2)}) collective-permute-start(bf16[32,768]{1,0:T(8,128)(2,1)S(1)} %out_project.1.refs_0_), channel_id=1, source_target_pairs={{0,12},{4,8},{8,4},{12,0},{1,13},{5,9},{9,5},{13,1},{2,14},{6,10},... | collective-permute-start | bytes 147464 | tf_op jit(solution)/shard_map/ppermute | solution.py:236
  34.3 5.0 %collective-permute-start.14 = (bf16[32,768]{1,0:T(8,128)(2,1)S(1)}, bf16[32,768]{1,0:T(8,128)(2,1)S(1)}, u32[]{:S(2)}, u32[]{:S(2)}) collective-permute-start(bf16[32,768]{1,0:T(8,128)(2,1)S(1)} %out_project.1.refs_0_), channel_id=1, source_target_pairs={{0,8},{4,12},{8,0},{12,4},{1,9},{5,13},{9,1},{13,5},{2,10},{6,14},... | collective-permute-start | bytes 147464 | tf_op jit(solution)/shard_map/ppermute | solution.py:236
  34.3 5.1 %collective-permute-start.13 = (bf16[32,768]{1,0:T(8,128)(2,1)S(1)}, bf16[32,768]{1,0:T(8,128)(2,1)S(1)}, u32[]{:S(2)}, u32[]{:S(2)}) collective-permute-start(bf16[32,768]{1,0:T(8,128)(2,1)S(1)} %out_project.1.refs_0_), channel_id=1, source_target_pairs={{0,4},{4,0},{8,12},{12,8},{1,5},{5,1},{9,13},{13,9},{2,6},{6,2},{1... | collective-permute-start | bytes 147464 | tf_op jit(solution)/shard_map/ppermute | solution.py:236
  39.4 6.7 %slice-start.3 = ((s8[25165824]{0:T(1024)(128)(4,1)}), s8[4194304]{0:T(1024)(128)(4,1)S(1)}, s32[]{:S(2)}) async-start(s8[25165824]{0:T(1024)(128)(4,1)} %bitcast.9), calls=%async_computation.3 | async-start | bytes 8388608
  39.4 6.7 %slice-start.4 = ((s8[25165824]{0:T(1024)(128)(4,1)}), s8[4194304]{0:T(1024)(128)(4,1)S(1)}, s32[]{:S(2)}) async-start(s8[25165824]{0:T(1024)(128)(4,1)} %bitcast.9), calls=%async_computation.4 | async-start | bytes 8388608
  39.4 6.7 %slice-start.5 = ((s8[25165824]{0:T(1024)(128)(4,1)}), s8[4194304]{0:T(1024)(128)(4,1)S(1)}, s32[]{:S(2)}) async-start(s8[25165824]{0:T(1024)(128)(4,1)} %bitcast.9), calls=%async_computation.5 | async-start | bytes 8388608
  39.4 6.7 %slice-start.10 = ((s8[25165824]{0:T(1024)(128)(4,1)}), s8[4194304]{0:T(1024)(128)(4,1)S(1)}, s32[]{:S(2)}) async-start(s8[25165824]{0:T(1024)(128)(4,1)} %bitcast.11), calls=%async_computation.10 | async-start | bytes 8388608
  39.4 7.0 %slice-start.11 = ((s8[25165824]{0:T(1024)(128)(4,1)}), s8[4194304]{0:T(1024)(128)(4,1)S(1)}, s32[]{:S(2)}) async-start(s8[25165824]{0:T(1024)(128)(4,1)} %bitcast.11), calls=%async_computation.11 | async-start | bytes 8388608
  40.0 4.7 %collective-permute-start.16 = (bf16[16,3072]{1,0:T(8,128)(2,1)S(1)}, bf16[16,3072]{1,0:T(8,128)(2,1)S(1)}, u32[]{:S(2)}, u32[]{:S(2)}) collective-permute-start(bf16[16,3072]{1,0:T(8,128)(2,1)S(1)} %get-tuple-element.38), channel_id=1, source_target_pairs={{0,2},{1,3},{2,0},{3,1},{4,6},{5,7},{6,4},{7,5},{8,10},{9,11},{10,... | collective-permute-start | bytes 294920 | tf_op jit(solution)/shard_map/ppermute | solution.py:236
  41.6 3.1 %collective-permute-start.17 = (bf16[16,3072]{1,0:T(8,128)(2,1)S(1)}, bf16[16,3072]{1,0:T(8,128)(2,1)S(1)}, u32[]{:S(2)}, u32[]{:S(2)}) collective-permute-start(bf16[16,3072]{1,0:T(8,128)(2,1)S(1)} %get-tuple-element.37.refs_0_), channel_id=1, source_target_pairs={{0,1},{1,0},{2,3},{3,2},{4,5},{5,4},{6,7},{7,6},{8,9},{9,8},{10,11... | collective-permute-start | bytes 294920 | tf_op jit(solution)/shard_map/ppermute | solution.py:236
  44.7 1.3 %collective-permute-start.18 = (bf16[16,3072]{1,0:T(8,128)(2,1)S(1)}, bf16[16,3072]{1,0:T(8,128)(2,1)S(1)}, u32[]{:S(2)}, u32[]{:S(2)}) collective-permute-start(bf16[16,3072]{1,0:T(8,128)(2,1)S(1)} %collective-permute-done.16.refs_1_), channel_id=1, source_target_pairs={{0,1},{1,0},{2,3},{3,2},{4,5},{5,4},{6,7},{7,6},{8,9},{9,8},{10,11... | collective-permute-start | bytes 294920 | tf_op jit(solution)/shard_map/ppermute | solution.py:236
  59.7 1.5 %collective-permute-start.19 = (bf16[32,3072]{1,0:T(8,128)(2,1)S(1)}, bf16[32,3072]{1,0:T(8,128)(2,1)S(1)}, u32[]{:S(2)}, u32[]{:S(2)}) collective-permute-start(bf16[32,3072]{1,0:T(8,128)(2,1)S(1)} %get-tuple-element.40), channel_id=1, source_target_pairs={{0,1},{1,0},{2,3},{3,2},{4,5},{5,4},{6,7},{7,6},{8,9},{9,8},{10,11... | collective-permute-start | bytes 589832 | tf_op jit(solution)/shard_map/ppermute | solution.py:236
  61.2 4.9 %collective-permute-start.20 = (bf16[16,3072]{1,0:T(8,128)(2,1)S(1)}, bf16[16,3072]{1,0:T(8,128)(2,1)S(1)}, u32[]{:S(2)}, u32[]{:S(2)}) collective-permute-start(bf16[16,3072]{1,0:T(8,128)(2,1)S(1)} %merge.1), channel_id=1, source_target_pairs={{0,2},{1,3},{2,0},{3,1},{4,6},{5,7},{6,4},{7,5},{8,10},{9,11},{10,... | collective-permute-start | bytes 294920 | tf_op jit(solution)/shard_map/ppermute | solution.py:236
  66.6 6.3 %collective-permute-start.21 = (bf16[8,3072]{1,0:T(8,128)(2,1)S(1)}, bf16[8,3072]{1,0:T(8,128)(2,1)S(1)}, u32[]{:S(2)}, u32[]{:S(2)}) collective-permute-start(bf16[8,3072]{1,0:T(8,128)(2,1)S(1)} %get-tuple-element.44), channel_id=1, source_target_pairs={{0,12},{4,8},{8,4},{12,0},{1,13},{5,9},{9,5},{13,1},{2,14},{6,10},... | collective-permute-start | bytes 147464 | tf_op jit(solution)/shard_map/ppermute | solution.py:236
  68.6 5.5 %collective-permute-start.22 = (bf16[8,3072]{1,0:T(8,128)(2,1)S(1)}, bf16[8,3072]{1,0:T(8,128)(2,1)S(1)}, u32[]{:S(2)}, u32[]{:S(2)}) collective-permute-start(bf16[8,3072]{1,0:T(8,128)(2,1)S(1)} %get-tuple-element.45), channel_id=1, source_target_pairs={{0,8},{4,12},{8,0},{12,4},{1,9},{5,13},{9,1},{13,5},{2,10},{6,14},... | collective-permute-start | bytes 147464 | tf_op jit(solution)/shard_map/ppermute | solution.py:236
  68.7 5.4 %collective-permute-start.23 = (bf16[8,3072]{1,0:T(8,128)(2,1)S(1)}, bf16[8,3072]{1,0:T(8,128)(2,1)S(1)}, u32[]{:S(2)}, u32[]{:S(2)}) collective-permute-start(bf16[8,3072]{1,0:T(8,128)(2,1)S(1)} %get-tuple-element.46), channel_id=1, source_target_pairs={{0,4},{4,0},{8,12},{12,8},{1,5},{5,1},{9,13},{13,9},{2,6},{6,2},{1... | collective-permute-start | bytes 147464 | tf_op jit(solution)/shard_map/ppermute | solution.py:236
where the time goes:
time: 74.9 us; the launch traced here: 74.8 us
  starting transfers between devices  28.3 us (38%)
  waiting for transfers between devices  26.5 us (35%)
  Pallas kernels  17.6 us (23%)
  local copies, waits for them, and re-layouts  1.12 us (1%)
  other arithmetic  0.89 us (1%)
    ppermute x20, starting transfers between devices, flip(): lax.ppermute(x, axis, [(i, i ^ mask) for i in range(lax.axis_size(axis))])  23.4 us
    ppermute x20, waiting for transfers between devices, flip(): lax.ppermute(x, axis, [(i, i ^ mask) for i in range(lax.axis_size(axis))])  22.4 us
    pallas_call x1, Pallas kernels, experts(): pl.pallas_call(kernel, out_shape=[pltpu.VMEM((slots, width), jnp.float32)...  13.2 us
    ppermute x3, waiting for transfers between devices, fast_layer(): lax.ppermute(payloads[shift], 'ctx', plan[2][shift])  4.1 us
    ppermute x1, starting transfers between devices, fast_layer(): one = lax.ppermute(packed[1], ('ctx', 'opt'), to_one)  3.09 us
    ppermute x3, starting transfers between devices, fast_layer(): lax.ppermute(payloads[shift], 'ctx', plan[2][shift])  1.79 us
  transfers between devices with their start and end apart: 24, of which 13 were waited for; matrix products, arithmetic and copies ran while one was open for 0% of the time, Pallas kernels for 2%

commit v1 on v0

--- a/solution.py
+++ b/solution.py
@@ -261,7 +261,6 @@
 
 MIB = 1 << 20
 STAGE_FLOPS = 8 * 10**9
-HEADS_ORDER = (1, 2, 3)
 EXPERT_MIB = 11
 
 
@@ -303,9 +302,8 @@
             sends.setdefault((head // tile_heads, dst), []).append(head)
     pairs = {}
     for shift in range(1, ctx_count):
-        found = [(s, (s + shift) % ctx_count) for s in range(ctx_count)]
-        found = [pair for pair in found if pair in sends]
-        if found:
+        found = [(s, s ^ shift) for s in range(ctx_count)]
+        if any(pair in sends for pair in found):
             pairs[shift] = found
     return wanted, sends, pairs
 
@@ -371,7 +369,7 @@
     heads = columns // HD
     _, sends, pairs = plan
     shifts = sorted(pairs)
-    widths = [max(len(sends[pair]) for pair in pairs[shift]) * HD for shift in shifts]
+    widths = [max(len(sends.get(pair, [])) for pair in pairs[shift]) * HD for shift in shifts]
     step = 4 * HD
 
     def kernel(*refs):
@@ -399,7 +397,7 @@
             @pl.when(here == s)
             def _():
                 for shift, payload_ref in zip(shifts, payload_refs):
-                    for place, head in enumerate(sends.get((s, (s + shift) % ctx_count), [])):
+                    for place, head in enumerate(sends.get((s, s ^ shift), [])):
                         local = (head - s * heads) * HD
                         payload_ref[:, place * HD : (place + 1) * HD] = tile_ref[:, local : local + HD]
 
@@ -439,7 +437,7 @@
                     if src == dst:
                         block, at = tile_ref, head - src * heads
                     else:
-                        block = arrived_refs[(dst - src) % ctx_count]
+                        block = arrived_refs[dst ^ src]
                         at = sends[(src, dst)].index(head)
                     mine_ref[:, place * HD : (place + 1) * HD] = block[:, at * HD : (at + 1) * HD]
 
@@ -474,13 +472,13 @@
             sums = sums + jnp.dot(low, value, preferred_element_type=jnp.float32)
         result = (sums / totals).astype(jnp.bfloat16)
         for place in range(group):
-            out_ref[:total, place * HD : (place + 1) * HD] = result[place * total : (place + 1) * total]
-        out_ref[total:, :] = jnp.zeros((rows, group * HD), jnp.bfloat16)
-        out_ref[total:, :HD] = numbers_ref[...]
+            out_ref[:, place * HD : (place + 1) * HD] = result[place * total : (place + 1) * total]
+        out_ref[:, group * HD :] = jnp.zeros((total, HD), jnp.bfloat16)
+        out_ref[:rows, group * HD :] = numbers_ref[...]
 
     return pl.pallas_call(
         kernel,
-        out_shape=jax.ShapeDtypeStruct((total + rows, group * HD), jnp.bfloat16),
+        out_shape=jax.ShapeDtypeStruct((total, (group + 1) * HD), jnp.bfloat16),
         in_specs=[whole()] * (2 + len(shifts) + len(passage_parts)),
         out_specs=whole(),
         scratch_shapes=[pltpu.VMEM((total, (group + 2) * HD), jnp.bfloat16)],
@@ -491,7 +489,7 @@
 
 
 def out_project(attention, weight, parts):
-    width = attention[0].shape[1]
+    width = attention[0].shape[1] - HD
     rows = parts[0].shape[0]
     ctx_count = len(parts)
     total = rows * ctx_count
@@ -506,7 +504,7 @@
         product = jnp.zeros((total, columns), jnp.float32)
         for k in range(ctx_count):
             product = product + jnp.dot(
-                attention_refs[k][:total, :],
+                attention_refs[k][:, :width],
                 weight_ref[aligned(here ^ k, width), :],
                 preferred_element_type=jnp.float32,
             )
@@ -541,7 +539,7 @@
         half = lax.axis_index("opt") // 2
         for k in range(ctx_count):
             full_ref[:, aligned(here ^ k, columns)] = mixed_refs[k][...].astype(jnp.float32)
-            ids_ref[aligned(here ^ k, rows), :] = id_refs[k][total:, :HD].astype(jnp.float32)
+            ids_ref[aligned(here ^ k, rows), :] = id_refs[k][:rows, -HD:].astype(jnp.float32)
         floats = full_ref[...]
         factor = lax.rsqrt(jnp.mean(floats * floats, axis=-1, keepdims=True) + EPS)
         expert_in = (floats * factor * gain_ref[...]).astype(jnp.bfloat16)
@@ -629,9 +627,15 @@
                 c = jnp.dot(hidden, down_ref[at, cut], preferred_element_type=jnp.float32)[:count]
                 total_ref[:, cut] = c if i == 0 else total_ref[:, cut] + c
 
+        def gate_of(i):
+            at = slice(i * tile, (i + 1) * tile)
+            return jnp.dot(rows_ref[...], gate_ref[:, at], preferred_element_type=jnp.float32)[:count]
+
+        ahead = gate_of(0)
         for i in range(ups.count):
-            at = slice(i * tile, (i + 1) * tile)
-            a = jnp.dot(rows_ref[...], gate_ref[:, at], preferred_element_type=jnp.float32)[:count]
+            a = ahead
+            if i + 1 < ups.count:
+                ahead = gate_of(i + 1)
             b = jnp.dot(rows_ref[...], ups.ready(i), preferred_element_type=jnp.float32)[:count]
             ups.start(i + ups.slots)
             if i > 0:
@@ -761,7 +765,9 @@
     third = flip(packed[2], "ctx", 3)
 
     product, payloads = project(parts, attention_gain, input_weight, cosine, sine, plan)
-    arrived = {shift: lax.ppermute(payloads[shift], "ctx", plan[2][shift]) for shift in HEADS_ORDER}
+    arrived = {}
+    for shift in payloads:
+        arrived[shift] = lax.ppermute(payloads[shift], "ctx", plan[2][shift])
     passage_parts = [packed[0], one, flip(one, "opt", 1), third, flip(third, "opt", 1)]
     attention = attend(product, arrived, passage_parts, packed[3], plan)
     attention = gathered(attention, "ctx")

time: 74.9 us -> 74 us (0.988)
  waiting for transfers between devices: 26.5 us -> 24.1 us
  starting transfers between devices: 28.3 us -> 30 us
    ppermute x20, waiting for transfers between devices: 22.4 us -> 20.1 us  [flip(): lax.ppermute(x, axis, [(i, i ^ mask) for i in range(lax.axis_size(axis))])]
    ppermute x3, starting transfers between devices: 1.79 us -> 3.55 us  [fast_layer(): arrived[shift] = lax.ppermute(payloads[shift], 'ctx', plan[2][shift])]
  transfers between devices with their start and end apart: 24 -> 24, of which waited for: 13 -> 12; matrix products, arithmetic and copies ran while one was open for 0% -> 0% of each run, Pallas kernels for 2% -> 2%
where the time goes in v1:
time: 74 us; the launch traced here: 73.8 us
  starting transfers between devices  30 us (41%)
  waiting for transfers between devices  24.1 us (33%)
  Pallas kernels  17.3 us (23%)
  local copies, waits for them, and re-layouts  1.12 us (2%)
  other arithmetic  0.89 us (1%)
    ppermute x20, starting transfers between devices, flip(): lax.ppermute(x, axis, [(i, i ^ mask) for i in range(lax.axis_size(axis))])  23.4 us
    ppermute x20, waiting for transfers between devices, flip(): lax.ppermute(x, axis, [(i, i ^ mask) for i in range(lax.axis_size(axis))])  20.1 us
    pallas_call x1, Pallas kernels, experts(): pl.pallas_call(kernel, out_shape=[pltpu.VMEM((slots, width), jnp.float32)...  12.9 us
    ppermute x3, waiting for transfers between devices, fast_layer(): arrived[shift] = lax.ppermute(payloads[shift], 'ctx', plan[2][shift])  4.04 us
    ppermute x3, starting transfers between devices, fast_layer(): arrived[shift] = lax.ppermute(payloads[shift], 'ctx', plan[2][shift])  3.55 us
    ppermute x1, starting transfers between devices, fast_layer(): one = lax.ppermute(packed[1], ('ctx', 'opt'), to_one)  3.09 us
  transfers between devices with their start and end apart: 24, of which 12 were waited for; matrix products, arithmetic and copies ran while one was open for 0% of the time, Pallas kernels for 2%

profile of v1, /device:TPU:0, one launch (start us, length us, event | category | flops | bytes accessed | tf_op | source)
XLA Modules:
  0.0 73.8 jit_solution(2434277089691339421)
XLA Ops:
  0.0 0.1 fusion.1
  0.2 0.1 pad_maximum_fusion
  0.3 0.0 copy-start.1
  0.3 0.4 copy-done.6
  0.7 0.2 copy-done.3
  0.9 0.1 copy-done.2
  1.0 0.1 pack.1
  1.1 3.1 %collective-permute-start.6 = (bf16[128,256]{1,0:T(8,128)(2,1)S(1)}, bf16[128,256]{1,0:T(8,128)(2,1)S(1)}, u32[]{:S(2)}, u32[]{:S(2)}) collective-permute-start(bf16[128,256]{1,0:T(8,128)(2,1)S(1)} %get-tuple-element.33), channel_id=1, source_target_pairs={{0,4},{1,9},{2,6},{3,11},{4,0},{5,13},{6,2},{7,15},{8,12},{9,1},{1... | collective-permute-start | bytes 196616 | tf_op jit(solution)/shard_map/ppermute | solution.py:764
  4.2 2.5 %collective-permute-start.2 = (bf16[8,3072]{1,0:T(8,128)(2,1)S(1)}, bf16[8,3072]{1,0:T(8,128)(2,1)S(1)}, u32[]{:S(2)}, u32[]{:S(2)}) collective-permute-start(bf16[8,3072]{1,0:T(8,128)(2,1)S(1)} %bitcast.15), channel_id=1, source_target_pairs={{0,12},{4,8},{8,4},{12,0},{1,13},{5,9},{9,5},{13,1},{2,14},{6,10},... | collective-permute-start | bytes 147464 | tf_op jit(solution)/shard_map/ppermute | solution.py:236
  6.6 0.1 collective-permute-start.1
  6.8 1.8 %collective-permute-start = (bf16[8,3072]{1,0:T(8,128)(2,1)S(1)}, bf16[8,3072]{1,0:T(8,128)(2,1)S(1)}, u32[]{:S(2)}, u32[]{:S(2)}) collective-permute-start(bf16[8,3072]{1,0:T(8,128)(2,1)S(1)} %bitcast.17), channel_id=1, source_target_pairs={{0,4},{4,0},{8,12},{12,8},{1,5},{5,1},{9,13},{13,9},{2,6},{6,2},{1... | collective-permute-start | bytes 147464 | tf_op jit(solution)/shard_map/ppermute | solution.py:236
  8.6 2.5 %collective-permute-start.8 = (bf16[64,256]{1,0:T(8,128)(2,1)S(1)}, bf16[64,256]{1,0:T(8,128)(2,1)S(1)}, u32[]{:S(2)}, u32[]{:S(2)}) collective-permute-start(bf16[64,256]{1,0:T(8,128)(2,1)S(1)} %get-tuple-element.34), channel_id=1, source_target_pairs={{0,12},{4,8},{8,4},{12,0},{1,13},{5,9},{9,5},{13,1},{2,14},{6,10},... | collective-permute-start | bytes 98312 | tf_op jit(solution)/shard_map/ppermute | solution.py:236
  11.0 0.0 collective-permute-start.7
  11.0 0.0 collective-permute-done.2.refs_3_.refs_8_
  11.0 1.6 %collective-permute-done.1.refs_2_.refs_7_ = bf16[8,3072]{1,0:T(8,128)(2,1)S(1)} collective-permute-done((bf16[8,3072]{1,0:T(8,128)(2,1)S(1)}, bf16[8,3072]{1,0:T(8,128)(2,1)S(1)}, u32[]{:S(2)}, u32[]{:S(2)}) %collective-permute-start.1) | collective-permute-done | bytes 49184 | tf_op jit(solution)/shard_map/ppermute | solution.py:236
  12.7 1.4 %project.1 = (bf16[32,1024]{1,0:T(8,128)(2,1)S(1)}, bf16[32,768]{1,0:T(8,128)(2,1)S(1)}, bf16[32,256]{1,0:T(8,128)(2,1)S(1)}, bf16[32,512]{1,0:T(8,128)(2,1)S(1)}) custom-call(bf16[8,3072]{1,0:T(8,128)(2,1)S(1)} %bitcast.18, bf16[8,3072]{1,0:T(8,128)(2,1)S(1)} %collective-permute-done.refs_1_.refs_6_, ...), custom_call_target="tpu_custom_call" | custom-call | bytes 6291456 | tf_op jit(solution)/shard_map/project/pallas_call | solution.py:404
  14.1 0.5 collective-permute-start.3
  14.6 0.0 collective-permute-done.8.refs_7_
  14.6 0.0 collective-permute-start.9
  14.6 2.5 %collective-permute-start.5 = (bf16[32,512]{1,0:T(8,128)(2,1)S(1)}, bf16[32,512]{1,0:T(8,128)(2,1)S(1)}, u32[]{:S(2)}, u32[]{:S(2)}) collective-permute-start(bf16[32,512]{1,0:T(8,128)(2,1)S(1)} %get-tuple-element.31), channel_id=1, source_target_pairs={{0,12},{4,8},{8,4},{12,0},{1,13},{5,9},{9,5},{13,1},{2,14},{6,10},... | collective-permute-start | bytes 98312 | tf_op jit(solution)/shard_map/ppermute | solution.py:770
  17.1 0.6 collective-permute-start.4
  17.7 4.0 %collective-permute-done.4.refs_2_ = bf16[32,256]{1,0:T(8,128)(2,1)S(1)} collective-permute-done((bf16[32,256]{1,0:T(8,128)(2,1)S(1)}, bf16[32,256]{1,0:T(8,128)(2,1)S(1)}, u32[]{:S(2)}, u32[]{:S(2)}) %collective-permute-start.4) | collective-permute-done | bytes 16416 | tf_op jit(solution)/shard_map/ppermute | solution.py:770
  21.7 0.0 collective-permute-done.5.refs_3_
  21.7 0.0 collective-permute-done.3.refs_1_
  21.8 0.0 slice-start.15
  21.8 0.0 copy-start.4
  21.8 0.0 copy-start.5
  21.8 0.0 slice-start.6
  21.8 0.0 slice-start.7
  21.8 0.9 %attend.1.refs_0_.refs_6_ = bf16[32,896]{1,0:T(8,128)(2,1)S(1)} custom-call(bf16[32,1024]{1,0:T(8,128)(2,1)S(1)} %get-tuple-element.28.refs_0_, bf16[32,768]{1,0:T(8,128)(2,1)S(1)} %collective-permute-done.3.refs_1_, bf16[32,256]{1,0:T(8,128)(2,1)S(1)} %collective-permute-done.4.refs_2_, bf16[32,512]{1,0:T(8,128)(2,1)S(1)} %collective-permute-done.5.refs_3_, ...), custom_call_target="tpu_custom_call" | custom-call | flops 8000000000 | tf_op jit(solution)/shard_map/attend/pallas_call | solution.py:479
  22.7 0.0 slice-start
  22.7 0.0 slice-start.1
  22.7 0.0 slice-start.2
  22.7 0.0 slice-start.8
  22.7 0.0 slice-start.9
  22.8 2.0 %collective-permute-start.12 = (bf16[32,896]{1,0:T(8,128)(2,1)S(1)}, bf16[32,896]{1,0:T(8,128)(2,1)S(1)}, u32[]{:S(2)}, u32[]{:S(2)}) collective-permute-start(bf16[32,896]{1,0:T(8,128)(2,1)S(1)} %attend.1.refs_0_.refs_6_), channel_id=1, source_target_pairs={{0,12},{4,8},{8,4},{12,0},{1,13},{5,9},{9,5},{13,1},{2,14},{6,10},... | collective-permute-start | bytes 172040 | tf_op jit(solution)/shard_map/ppermute | solution.py:236
  24.7 0.5 collective-permute-start.11
  25.2 2.0 %collective-permute-start.10 = (bf16[32,896]{1,0:T(8,128)(2,1)S(1)}, bf16[32,896]{1,0:T(8,128)(2,1)S(1)}, u32[]{:S(2)}, u32[]{:S(2)}) collective-permute-start(bf16[32,896]{1,0:T(8,128)(2,1)S(1)} %attend.1.refs_0_.refs_6_), channel_id=1, source_target_pairs={{0,4},{4,0},{8,12},{12,8},{1,5},{5,1},{9,13},{13,9},{2,6},{6,2},{1... | collective-permute-start | bytes 172040 | tf_op jit(solution)/shard_map/ppermute | solution.py:236
  27.2 1.8 %collective-permute-done.12.refs_3_.refs_9_ = bf16[32,896]{1,0:T(8,128)(2,1)S(1)} collective-permute-done((bf16[32,896]{1,0:T(8,128)(2,1)S(1)}, bf16[32,896]{1,0:T(8,128)(2,1)S(1)}, u32[]{:S(2)}, u32[]{:S(2)}) %collective-permute-start.12) | collective-permute-done | bytes 57376 | tf_op jit(solution)/shard_map/ppermute | solution.py:236
  29.0 1.5 %collective-permute-done.11.refs_2_.refs_8_ = bf16[32,896]{1,0:T(8,128)(2,1)S(1)} collective-permute-done((bf16[32,896]{1,0:T(8,128)(2,1)S(1)}, bf16[32,896]{1,0:T(8,128)(2,1)S(1)}, u32[]{:S(2)}, u32[]{:S(2)}) %collective-permute-start.11) | collective-permute-done | bytes 57376 | tf_op jit(solution)/shard_map/ppermute | solution.py:236
  30.5 0.9 %out_project.1.refs_0_ = bf16[32,768]{1,0:T(8,128)(2,1)S(1)} custom-call(bf16[32,896]{1,0:T(8,128)(2,1)S(1)} %attend.1.refs_0_.refs_6_, bf16[32,896]{1,0:T(8,128)(2,1)S(1)} %collective-permute-done.10.refs_1_.refs_7_, bf16[32,896]{1,0:T(8,128)(2,1)S(1)} %collective-permute-done.11.refs_2_.refs_8_, ...), custom_call_target="tpu_custom_call" | custom-call | flops 8000000000 | bytes 4718592 | tf_op jit(solution)/shard_map/out_project/pallas_call | solution.py:514
  31.4 2.0 %collective-permute-start.15 = (bf16[32,768]{1,0:T(8,128)(2,1)S(1)}, bf16[32,768]{1,0:T(8,128)(2,1)S(1)}, u32[]{:S(2)}, u32[]{:S(2)}) collective-permute-start(bf16[32,768]{1,0:T(8,128)(2,1)S(1)} %out_project.1.refs_0_), channel_id=1, source_target_pairs={{0,12},{4,8},{8,4},{12,0},{1,13},{5,9},{9,5},{13,1},{2,14},{6,10},... | collective-permute-start | bytes 147464 | tf_op jit(solution)/shard_map/ppermute | solution.py:236
  33.5 0.4 collective-permute-start.14
  33.8 2.0 %collective-permute-start.13 = (bf16[32,768]{1,0:T(8,128)(2,1)S(1)}, bf16[32,768]{1,0:T(8,128)(2,1)S(1)}, u32[]{:S(2)}, u32[]{:S(2)}) collective-permute-start(bf16[32,768]{1,0:T(8,128)(2,1)S(1)} %out_project.1.refs_0_), channel_id=1, source_target_pairs={{0,4},{4,0},{8,12},{12,8},{1,5},{5,1},{9,13},{13,9},{2,6},{6,2},{1... | collective-permute-start | bytes 147464 | tf_op jit(solution)/shard_map/ppermute | solution.py:236
  35.9 1.8 %collective-permute-done.15.refs_3_ = bf16[32,768]{1,0:T(8,128)(2,1)S(1)} collective-permute-done((bf16[32,768]{1,0:T(8,128)(2,1)S(1)}, bf16[32,768]{1,0:T(8,128)(2,1)S(1)}, u32[]{:S(2)}, u32[]{:S(2)}) %collective-permute-start.15) | collective-permute-done | bytes 49184 | tf_op jit(solution)/shard_map/ppermute | solution.py:236
  37.7 1.2 %collective-permute-done.14.refs_2_ = bf16[32,768]{1,0:T(8,128)(2,1)S(1)} collective-permute-done((bf16[32,768]{1,0:T(8,128)(2,1)S(1)}, bf16[32,768]{1,0:T(8,128)(2,1)S(1)}, u32[]{:S(2)}, u32[]{:S(2)}) %collective-permute-start.14) | collective-permute-done | bytes 49184 | tf_op jit(solution)/shard_map/ppermute | solution.py:236
  38.9 0.0 slice-start.10
  38.9 0.6 route.1
  39.5 1.5 %collective-permute-start.16 = (bf16[16,3072]{1,0:T(8,128)(2,1)S(1)}, bf16[16,3072]{1,0:T(8,128)(2,1)S(1)}, u32[]{:S(2)}, u32[]{:S(2)}) collective-permute-start(bf16[16,3072]{1,0:T(8,128)(2,1)S(1)} %get-tuple-element.38), channel_id=1, source_target_pairs={{0,2},{1,3},{2,0},{3,1},{4,6},{5,7},{6,4},{7,5},{8,10},{9,11},{10,... | collective-permute-start | bytes 294920 | tf_op jit(solution)/shard_map/ppermute | solution.py:236
  41.1 3.1 %collective-permute-done.16.refs_1_ = bf16[16,3072]{1,0:T(8,128)(2,1)S(1)} collective-permute-done((bf16[16,3072]{1,0:T(8,128)(2,1)S(1)}, bf16[16,3072]{1,0:T(8,128)(2,1)S(1)}, u32[]{:S(2)}, u32[]{:S(2)}) %collective-permute-start.16) | collective-permute-done | bytes 98336 | tf_op jit(solution)/shard_map/ppermute | solution.py:236
  44.2 1.3 %collective-permute-done.18.refs_3_ = bf16[16,3072]{1,0:T(8,128)(2,1)S(1)} collective-permute-done((bf16[16,3072]{1,0:T(8,128)(2,1)S(1)}, bf16[16,3072]{1,0:T(8,128)(2,1)S(1)}, u32[]{:S(2)}, u32[]{:S(2)}) %collective-permute-start.18) | collective-permute-done | bytes 98336 | tf_op jit(solution)/shard_map/ppermute | solution.py:236
  45.6 0.3 slice-done.11
  45.9 12.9 %experts.1 = (f32[16,3072]{1,0:T(8,128)S(1)}, f32[16,3072]{1,0:T(8,128)S(1)}, bf16[32,3072]{1,0:T(8,128)(2,1)S(1)}) custom-call(bf16[16,3072]{1,0:T(8,128)(2,1)S(1)} %get-tuple-element.37.refs_0_, bf16[16,3072]{1,0:T(8,128)(2,1)S(1)} %collective-permute-done.16.refs_1_, bf16[16,3072]{1,0:T(8,128)(2,1)S(1)} %collective-permute-done.17.refs_2_, ...), custom_call_target="tpu_custom_call" | custom-call | flops 4831838208 | bytes 75497472 | tf_op jit(solution)/shard_map/experts/pallas_call | solution.py:651
  58.8 0.1 collective-permute-start.19
  58.9 1.4 %collective-permute-done.19.core_ref = bf16[32,3072]{1,0:T(8,128)(2,1)S(1)} collective-permute-done((bf16[32,3072]{1,0:T(8,128)(2,1)S(1)}, bf16[32,3072]{1,0:T(8,128)(2,1)S(1)}, u32[]{:S(2)}, u32[]{:S(2)}) %collective-permute-start.19) | collective-permute-done | bytes 196640 | tf_op jit(solution)/shard_map/ppermute | solution.py:236
  60.4 1.5 %collective-permute-start.20 = (bf16[16,3072]{1,0:T(8,128)(2,1)S(1)}, bf16[16,3072]{1,0:T(8,128)(2,1)S(1)}, u32[]{:S(2)}, u32[]{:S(2)}) collective-permute-start(bf16[16,3072]{1,0:T(8,128)(2,1)S(1)} %merge.1), channel_id=1, source_target_pairs={{0,2},{1,3},{2,0},{3,1},{4,6},{5,7},{6,4},{7,5},{8,10},{9,11},{10,... | collective-permute-start | bytes 294920 | tf_op jit(solution)/shard_map/ppermute | solution.py:236
  61.9 3.4 %collective-permute-done.20.back_ref = bf16[16,3072]{1,0:T(8,128)(2,1)S(1)} collective-permute-done((bf16[16,3072]{1,0:T(8,128)(2,1)S(1)}, bf16[16,3072]{1,0:T(8,128)(2,1)S(1)}, u32[]{:S(2)}, u32[]{:S(2)}) %collective-permute-start.20) | collective-permute-done | bytes 98336 | tf_op jit(solution)/shard_map/ppermute | solution.py:236
  65.3 0.5 combine.1
  65.7 2.0 %collective-permute-start.21 = (bf16[8,3072]{1,0:T(8,128)(2,1)S(1)}, bf16[8,3072]{1,0:T(8,128)(2,1)S(1)}, u32[]{:S(2)}, u32[]{:S(2)}) collective-permute-start(bf16[8,3072]{1,0:T(8,128)(2,1)S(1)} %get-tuple-element.44), channel_id=1, source_target_pairs={{0,12},{4,8},{8,4},{12,0},{1,13},{5,9},{9,5},{13,1},{2,14},{6,10},... | collective-permute-start | bytes 147464 | tf_op jit(solution)/shard_map/ppermute | solution.py:236
  67.8 0.6 collective-permute-start.22
  68.4 1.8 %collective-permute-start.23 = (bf16[8,3072]{1,0:T(8,128)(2,1)S(1)}, bf16[8,3072]{1,0:T(8,128)(2,1)S(1)}, u32[]{:S(2)}, u32[]{:S(2)}) collective-permute-start(bf16[8,3072]{1,0:T(8,128)(2,1)S(1)} %get-tuple-element.46), channel_id=1, source_target_pairs={{0,4},{4,0},{8,12},{12,8},{1,5},{5,1},{9,13},{13,9},{2,6},{6,2},{1... | collective-permute-start | bytes 147464 | tf_op jit(solution)/shard_map/ppermute | solution.py:236
  70.2 1.8 %collective-permute-done.21 = bf16[8,3072]{1,0:T(8,128)(2,1)S(1)} collective-permute-done((bf16[8,3072]{1,0:T(8,128)(2,1)S(1)}, bf16[8,3072]{1,0:T(8,128)(2,1)S(1)}, u32[]{:S(2)}, u32[]{:S(2)}) %collective-permute-start.21) | collective-permute-done | bytes 49184 | tf_op jit(solution)/shard_map/ppermute | solution.py:236
  72.0 1.2 %collective-permute-done.22 = bf16[8,3072]{1,0:T(8,128)(2,1)S(1)} collective-permute-done((bf16[8,3072]{1,0:T(8,128)(2,1)S(1)}, bf16[8,3072]{1,0:T(8,128)(2,1)S(1)}, u32[]{:S(2)}, u32[]{:S(2)}) %collective-permute-start.22) | collective-permute-done | bytes 49184 | tf_op jit(solution)/shard_map/ppermute | solution.py:236
  73.2 0.7 fusion
  (48 shorter events, 0.1 us)
Async XLA Ops:
  0.0 0.7 copy-start.6
  0.0 0.9 %copy-start.3 = (bf16[128,512]{1,0:T(8,128)(2,1)S(1)}, bf16[128,512]{1,0:T(8,128)(2,1)}, u32[]{:S(2)}) copy-start(bf16[128,512]{1,0:T(8,128)(2,1)} %values_ref.1) | copy-start | bytes 393220
  0.0 1.0 %copy-start.2 = (bf16[128,512]{1,0:T(8,128)(2,1)S(1)}, bf16[128,512]{1,0:T(8,128)(2,1)}, u32[]{:S(2)}) copy-start(bf16[128,512]{1,0:T(8,128)(2,1)} %keys_ref.1) | copy-start | bytes 393220
  0.3 3.9 %copy-start = (bf16[1,8,3072]{2,1,0:T(8,128)(2,1)S(1)}, bf16[1,8,3072]{2,1,0:T(8,128)(2,1)}, u32[]{:S(2)}) copy-start(bf16[1,8,3072]{2,1,0:T(8,128)(2,1)} %param.12) | copy-start | bytes 147460
  0.3 12.4 %slice-start.12 = ((s8[6291456]{0:T(1024)(128)(4,1)}), s8[4194304]{0:T(1024)(128)(4,1)S(1)}, s32[]{:S(2)}) async-start(s8[6291456]{0:T(1024)(128)(4,1)} %bitcast.13), calls=%async_computation.12 | async-start | bytes 8388608
  0.3 12.4 %copy-start.1 = (f32[3072]{0:T(1024)S(1)}, f32[3072]{0:T(1024)}, u32[]{:S(2)}) copy-start(f32[3072]{0:T(1024)} %param.15) | copy-start | bytes 36868
  1.0 11.7 %slice-start.13 = ((s8[6291456]{0:T(1024)(128)(4,1)}), s8[2097152]{0:T(1024)(128)(4,1)S(1)}, s32[]{:S(2)}) async-start(s8[6291456]{0:T(1024)(128)(4,1)} %bitcast.13), calls=%async_computation.13 | async-start | bytes 4194304
  1.1 29.4 %slice-start.14 = ((s8[4718592]{0:T(1024)(128)(4,1)}), s8[4194304]{0:T(1024)(128)(4,1)S(1)}, s32[]{:S(2)}) async-start(s8[4718592]{0:T(1024)(128)(4,1)} %bitcast.21), calls=%async_computation.14 | async-start | bytes 8388608
  1.1 10.0 %collective-permute-start.6 = (bf16[128,256]{1,0:T(8,128)(2,1)S(1)}, bf16[128,256]{1,0:T(8,128)(2,1)S(1)}, u32[]{:S(2)}, u32[]{:S(2)}) collective-permute-start(bf16[128,256]{1,0:T(8,128)(2,1)S(1)} %get-tuple-element.33), channel_id=1, source_target_pairs={{0,4},{1,9},{2,6},{3,11},{4,0},{5,13},{6,2},{7,15},{8,12},{9,1},{1... | collective-permute-start | bytes 196616 | tf_op jit(solution)/shard_map/ppermute | solution.py:764
  4.2 6.9 %collective-permute-start.2 = (bf16[8,3072]{1,0:T(8,128)(2,1)S(1)}, bf16[8,3072]{1,0:T(8,128)(2,1)S(1)}, u32[]{:S(2)}, u32[]{:S(2)}) collective-permute-start(bf16[8,3072]{1,0:T(8,128)(2,1)S(1)} %bitcast.15), channel_id=1, source_target_pairs={{0,12},{4,8},{8,4},{12,0},{1,13},{5,9},{9,5},{13,1},{2,14},{6,10},... | collective-permute-start | bytes 147464 | tf_op jit(solution)/shard_map/ppermute | solution.py:236
  6.6 6.0 %collective-permute-start.1 = (bf16[8,3072]{1,0:T(8,128)(2,1)S(1)}, bf16[8,3072]{1,0:T(8,128)(2,1)S(1)}, u32[]{:S(2)}, u32[]{:S(2)}) collective-permute-start(bf16[8,3072]{1,0:T(8,128)(2,1)S(1)} %bitcast.16), channel_id=1, source_target_pairs={{0,8},{4,12},{8,0},{12,4},{1,9},{5,13},{9,1},{13,5},{2,10},{6,14},... | collective-permute-start | bytes 147464 | tf_op jit(solution)/shard_map/ppermute | solution.py:236
  6.8 5.9 %collective-permute-start = (bf16[8,3072]{1,0:T(8,128)(2,1)S(1)}, bf16[8,3072]{1,0:T(8,128)(2,1)S(1)}, u32[]{:S(2)}, u32[]{:S(2)}) collective-permute-start(bf16[8,3072]{1,0:T(8,128)(2,1)S(1)} %bitcast.17), channel_id=1, source_target_pairs={{0,4},{4,0},{8,12},{12,8},{1,5},{5,1},{9,13},{13,9},{2,6},{6,2},{1... | collective-permute-start | bytes 147464 | tf_op jit(solution)/shard_map/ppermute | solution.py:236
  8.6 6.1 %collective-permute-start.8 = (bf16[64,256]{1,0:T(8,128)(2,1)S(1)}, bf16[64,256]{1,0:T(8,128)(2,1)S(1)}, u32[]{:S(2)}, u32[]{:S(2)}) collective-permute-start(bf16[64,256]{1,0:T(8,128)(2,1)S(1)} %get-tuple-element.34), channel_id=1, source_target_pairs={{0,12},{4,8},{8,4},{12,0},{1,13},{5,9},{9,5},{13,1},{2,14},{6,10},... | collective-permute-start | bytes 98312 | tf_op jit(solution)/shard_map/ppermute | solution.py:236
  11.0 10.7 %collective-permute-start.7 = (bf16[128,256]{1,0:T(8,128)(2,1)S(1)}, bf16[128,256]{1,0:T(8,128)(2,1)S(1)}, u32[]{:S(2)}, u32[]{:S(2)}) collective-permute-start(bf16[128,256]{1,0:T(8,128)(2,1)S(1)} %collective-permute-done.6.refs_5_), channel_id=1, source_target_pairs={{0,1},{1,0},{2,3},{3,2},{4,5},{5,4},{6,7},{7,6},{8,9},{9,8},{10,11... | collective-permute-start | bytes 196616 | tf_op jit(solution)/shard_map/ppermute | solution.py:236
  14.1 7.6 %collective-permute-start.3 = (bf16[32,768]{1,0:T(8,128)(2,1)S(1)}, bf16[32,768]{1,0:T(8,128)(2,1)S(1)}, u32[]{:S(2)}, u32[]{:S(2)}) collective-permute-start(bf16[32,768]{1,0:T(8,128)(2,1)S(1)} %get-tuple-element.29), channel_id=1, source_target_pairs={{0,4},{4,0},{8,12},{12,8},{1,5},{5,1},{9,13},{13,9},{2,6},{6,2},{1... | collective-permute-start | bytes 147464 | tf_op jit(solution)/shard_map/ppermute | solution.py:770
  14.6 7.1 %collective-permute-start.9 = (bf16[64,256]{1,0:T(8,128)(2,1)S(1)}, bf16[64,256]{1,0:T(8,128)(2,1)S(1)}, u32[]{:S(2)}, u32[]{:S(2)}) collective-permute-start(bf16[64,256]{1,0:T(8,128)(2,1)S(1)} %collective-permute-done.8.refs_7_), channel_id=1, source_target_pairs={{0,1},{1,0},{2,3},{3,2},{4,5},{5,4},{6,7},{7,6},{8,9},{9,8},{10,11... | collective-permute-start | bytes 98312 | tf_op jit(solution)/shard_map/ppermute | solution.py:236
  14.6 7.1 %collective-permute-start.5 = (bf16[32,512]{1,0:T(8,128)(2,1)S(1)}, bf16[32,512]{1,0:T(8,128)(2,1)S(1)}, u32[]{:S(2)}, u32[]{:S(2)}) collective-permute-start(bf16[32,512]{1,0:T(8,128)(2,1)S(1)} %get-tuple-element.31), channel_id=1, source_target_pairs={{0,12},{4,8},{8,4},{12,0},{1,13},{5,9},{9,5},{13,1},{2,14},{6,10},... | collective-permute-start | bytes 98312 | tf_op jit(solution)/shard_map/ppermute | solution.py:770
  17.1 4.6 %collective-permute-start.4 = (bf16[32,256]{1,0:T(8,128)(2,1)S(1)}, bf16[32,256]{1,0:T(8,128)(2,1)S(1)}, u32[]{:S(2)}, u32[]{:S(2)}) collective-permute-start(bf16[32,256]{1,0:T(8,128)(2,1)S(1)} %get-tuple-element.30), channel_id=1, source_target_pairs={{0,8},{4,12},{8,0},{12,4},{1,9},{5,13},{9,1},{13,5},{2,10},{6,14},... | collective-permute-start | bytes 49160 | tf_op jit(solution)/shard_map/ppermute | solution.py:770
  21.8 8.7 %slice-start.15 = ((s8[4718592]{0:T(1024)(128)(4,1)}), s8[524288]{0:T(1024)(128)(4,1)S(1)}, s32[]{:S(2)}) async-start(s8[4718592]{0:T(1024)(128)(4,1)} %bitcast.21), calls=%async_computation.15 | async-start | bytes 1048576
  21.8 17.1 %copy-start.4 = (bf16[3072,8]{0,1:T(8,128)(2,1)S(1)}, bf16[3072,8]{0,1:T(8,128)(2,1)}, u32[]{:S(2)}) copy-start(bf16[3072,8]{0,1:T(8,128)(2,1)} %param.19) | copy-start | bytes 147460
  21.8 17.1 %copy-start.5 = (f32[3072]{0:T(1024)S(1)}, f32[3072]{0:T(1024)}, u32[]{:S(2)}) copy-start(f32[3072]{0:T(1024)} %param.16) | copy-start | bytes 36868
  21.8 23.7 %slice-start.6 = ((s8[25165824]{0:T(1024)(128)(4,1)}), s8[4194304]{0:T(1024)(128)(4,1)S(1)}, s32[]{:S(2)}) async-start(s8[25165824]{0:T(1024)(128)(4,1)} %bitcast.11), calls=%async_computation.6 | async-start | bytes 8388608
  21.8 23.7 %slice-start.7 = ((s8[25165824]{0:T(1024)(128)(4,1)}), s8[4194304]{0:T(1024)(128)(4,1)S(1)}, s32[]{:S(2)}) async-start(s8[25165824]{0:T(1024)(128)(4,1)} %bitcast.11), calls=%async_computation.7 | async-start | bytes 8388608
  22.7 22.8 %slice-start = ((s8[25165824]{0:T(1024)(128)(4,1)}), s8[4194304]{0:T(1024)(128)(4,1)S(1)}, s32[]{:S(2)}) async-start(s8[25165824]{0:T(1024)(128)(4,1)} %bitcast.9), calls=%async_computation | async-start | bytes 8388608
  22.7 22.8 %slice-start.1 = ((s8[25165824]{0:T(1024)(128)(4,1)}), s8[4194304]{0:T(1024)(128)(4,1)S(1)}, s32[]{:S(2)}) async-start(s8[25165824]{0:T(1024)(128)(4,1)} %bitcast.9), calls=%async_computation.1 | async-start | bytes 8388608
  22.7 22.8 %slice-start.2 = ((s8[25165824]{0:T(1024)(128)(4,1)}), s8[4194304]{0:T(1024)(128)(4,1)S(1)}, s32[]{:S(2)}) async-start(s8[25165824]{0:T(1024)(128)(4,1)} %bitcast.9), calls=%async_computation.2 | async-start | bytes 8388608
  22.7 22.8 %slice-start.8 = ((s8[25165824]{0:T(1024)(128)(4,1)}), s8[4194304]{0:T(1024)(128)(4,1)S(1)}, s32[]{:S(2)}) async-start(s8[25165824]{0:T(1024)(128)(4,1)} %bitcast.11), calls=%async_computation.8 | async-start | bytes 8388608
  22.7 22.8 %slice-start.9 = ((s8[25165824]{0:T(1024)(128)(4,1)}), s8[4194304]{0:T(1024)(128)(4,1)S(1)}, s32[]{:S(2)}) async-start(s8[25165824]{0:T(1024)(128)(4,1)} %bitcast.11), calls=%async_computation.9 | async-start | bytes 8388608
  22.8 6.2 %collective-permute-start.12 = (bf16[32,896]{1,0:T(8,128)(2,1)S(1)}, bf16[32,896]{1,0:T(8,128)(2,1)S(1)}, u32[]{:S(2)}, u32[]{:S(2)}) collective-permute-start(bf16[32,896]{1,0:T(8,128)(2,1)S(1)} %attend.1.refs_0_.refs_6_), channel_id=1, source_target_pairs={{0,12},{4,8},{8,4},{12,0},{1,13},{5,9},{9,5},{13,1},{2,14},{6,10},... | collective-permute-start | bytes 172040 | tf_op jit(solution)/shard_map/ppermute | solution.py:236
  24.7 5.8 %collective-permute-start.11 = (bf16[32,896]{1,0:T(8,128)(2,1)S(1)}, bf16[32,896]{1,0:T(8,128)(2,1)S(1)}, u32[]{:S(2)}, u32[]{:S(2)}) collective-permute-start(bf16[32,896]{1,0:T(8,128)(2,1)S(1)} %attend.1.refs_0_.refs_6_), channel_id=1, source_target_pairs={{0,8},{4,12},{8,0},{12,4},{1,9},{5,13},{9,1},{13,5},{2,10},{6,14},... | collective-permute-start | bytes 172040 | tf_op jit(solution)/shard_map/ppermute | solution.py:236
  25.2 5.3 %collective-permute-start.10 = (bf16[32,896]{1,0:T(8,128)(2,1)S(1)}, bf16[32,896]{1,0:T(8,128)(2,1)S(1)}, u32[]{:S(2)}, u32[]{:S(2)}) collective-permute-start(bf16[32,896]{1,0:T(8,128)(2,1)S(1)} %attend.1.refs_0_.refs_6_), channel_id=1, source_target_pairs={{0,4},{4,0},{8,12},{12,8},{1,5},{5,1},{9,13},{13,9},{2,6},{6,2},{1... | collective-permute-start | bytes 172040 | tf_op jit(solution)/shard_map/ppermute | solution.py:236
  31.4 6.2 %collective-permute-start.15 = (bf16[32,768]{1,0:T(8,128)(2,1)S(1)}, bf16[32,768]{1,0:T(8,128)(2,1)S(1)}, u32[]{:S(2)}, u32[]{:S(2)}) collective-permute-start(bf16[32,768]{1,0:T(8,128)(2,1)S(1)} %out_project.1.refs_0_), channel_id=1, source_target_pairs={{0,12},{4,8},{8,4},{12,0},{1,13},{5,9},{9,5},{13,1},{2,14},{6,10},... | collective-permute-start | bytes 147464 | tf_op jit(solution)/shard_map/ppermute | solution.py:236
  33.5 5.4 %collective-permute-start.14 = (bf16[32,768]{1,0:T(8,128)(2,1)S(1)}, bf16[32,768]{1,0:T(8,128)(2,1)S(1)}, u32[]{:S(2)}, u32[]{:S(2)}) collective-permute-start(bf16[32,768]{1,0:T(8,128)(2,1)S(1)} %out_project.1.refs_0_), channel_id=1, source_target_pairs={{0,8},{4,12},{8,0},{12,4},{1,9},{5,13},{9,1},{13,5},{2,10},{6,14},... | collective-permute-start | bytes 147464 | tf_op jit(solution)/shard_map/ppermute | solution.py:236
  33.8 5.0 %collective-permute-start.13 = (bf16[32,768]{1,0:T(8,128)(2,1)S(1)}, bf16[32,768]{1,0:T(8,128)(2,1)S(1)}, u32[]{:S(2)}, u32[]{:S(2)}) collective-permute-start(bf16[32,768]{1,0:T(8,128)(2,1)S(1)} %out_project.1.refs_0_), channel_id=1, source_target_pairs={{0,4},{4,0},{8,12},{12,8},{1,5},{5,1},{9,13},{13,9},{2,6},{6,2},{1... | collective-permute-start | bytes 147464 | tf_op jit(solution)/shard_map/ppermute | solution.py:236
  38.9 6.7 %slice-start.3 = ((s8[25165824]{0:T(1024)(128)(4,1)}), s8[4194304]{0:T(1024)(128)(4,1)S(1)}, s32[]{:S(2)}) async-start(s8[25165824]{0:T(1024)(128)(4,1)} %bitcast.9), calls=%async_computation.3 | async-start | bytes 8388608
  38.9 6.7 %slice-start.4 = ((s8[25165824]{0:T(1024)(128)(4,1)}), s8[4194304]{0:T(1024)(128)(4,1)S(1)}, s32[]{:S(2)}) async-start(s8[25165824]{0:T(1024)(128)(4,1)} %bitcast.9), calls=%async_computation.4 | async-start | bytes 8388608
  38.9 6.7 %slice-start.5 = ((s8[25165824]{0:T(1024)(128)(4,1)}), s8[4194304]{0:T(1024)(128)(4,1)S(1)}, s32[]{:S(2)}) async-start(s8[25165824]{0:T(1024)(128)(4,1)} %bitcast.9), calls=%async_computation.5 | async-start | bytes 8388608
  38.9 6.7 %slice-start.10 = ((s8[25165824]{0:T(1024)(128)(4,1)}), s8[4194304]{0:T(1024)(128)(4,1)S(1)}, s32[]{:S(2)}) async-start(s8[25165824]{0:T(1024)(128)(4,1)} %bitcast.11), calls=%async_computation.10 | async-start | bytes 8388608
  38.9 7.0 %slice-start.11 = ((s8[25165824]{0:T(1024)(128)(4,1)}), s8[4194304]{0:T(1024)(128)(4,1)S(1)}, s32[]{:S(2)}) async-start(s8[25165824]{0:T(1024)(128)(4,1)} %bitcast.11), calls=%async_computation.11 | async-start | bytes 8388608
  39.5 4.7 %collective-permute-start.16 = (bf16[16,3072]{1,0:T(8,128)(2,1)S(1)}, bf16[16,3072]{1,0:T(8,128)(2,1)S(1)}, u32[]{:S(2)}, u32[]{:S(2)}) collective-permute-start(bf16[16,3072]{1,0:T(8,128)(2,1)S(1)} %get-tuple-element.38), channel_id=1, source_target_pairs={{0,2},{1,3},{2,0},{3,1},{4,6},{5,7},{6,4},{7,5},{8,10},{9,11},{10,... | collective-permute-start | bytes 294920 | tf_op jit(solution)/shard_map/ppermute | solution.py:236
  41.1 3.1 %collective-permute-start.17 = (bf16[16,3072]{1,0:T(8,128)(2,1)S(1)}, bf16[16,3072]{1,0:T(8,128)(2,1)S(1)}, u32[]{:S(2)}, u32[]{:S(2)}) collective-permute-start(bf16[16,3072]{1,0:T(8,128)(2,1)S(1)} %get-tuple-element.37.refs_0_), channel_id=1, source_target_pairs={{0,1},{1,0},{2,3},{3,2},{4,5},{5,4},{6,7},{7,6},{8,9},{9,8},{10,11... | collective-permute-start | bytes 294920 | tf_op jit(solution)/shard_map/ppermute | solution.py:236
  44.2 1.3 %collective-permute-start.18 = (bf16[16,3072]{1,0:T(8,128)(2,1)S(1)}, bf16[16,3072]{1,0:T(8,128)(2,1)S(1)}, u32[]{:S(2)}, u32[]{:S(2)}) collective-permute-start(bf16[16,3072]{1,0:T(8,128)(2,1)S(1)} %collective-permute-done.16.refs_1_), channel_id=1, source_target_pairs={{0,1},{1,0},{2,3},{3,2},{4,5},{5,4},{6,7},{7,6},{8,9},{9,8},{10,11... | collective-permute-start | bytes 294920 | tf_op jit(solution)/shard_map/ppermute | solution.py:236
  58.8 1.5 %collective-permute-start.19 = (bf16[32,3072]{1,0:T(8,128)(2,1)S(1)}, bf16[32,3072]{1,0:T(8,128)(2,1)S(1)}, u32[]{:S(2)}, u32[]{:S(2)}) collective-permute-start(bf16[32,3072]{1,0:T(8,128)(2,1)S(1)} %get-tuple-element.40), channel_id=1, source_target_pairs={{0,1},{1,0},{2,3},{3,2},{4,5},{5,4},{6,7},{7,6},{8,9},{9,8},{10,11... | collective-permute-start | bytes 589832 | tf_op jit(solution)/shard_map/ppermute | solution.py:236
  60.4 4.9 %collective-permute-start.20 = (bf16[16,3072]{1,0:T(8,128)(2,1)S(1)}, bf16[16,3072]{1,0:T(8,128)(2,1)S(1)}, u32[]{:S(2)}, u32[]{:S(2)}) collective-permute-start(bf16[16,3072]{1,0:T(8,128)(2,1)S(1)} %merge.1), channel_id=1, source_target_pairs={{0,2},{1,3},{2,0},{3,1},{4,6},{5,7},{6,4},{7,5},{8,10},{9,11},{10,... | collective-permute-start | bytes 294920 | tf_op jit(solution)/shard_map/ppermute | solution.py:236
  65.7 6.2 %collective-permute-start.21 = (bf16[8,3072]{1,0:T(8,128)(2,1)S(1)}, bf16[8,3072]{1,0:T(8,128)(2,1)S(1)}, u32[]{:S(2)}, u32[]{:S(2)}) collective-permute-start(bf16[8,3072]{1,0:T(8,128)(2,1)S(1)} %get-tuple-element.44), channel_id=1, source_target_pairs={{0,12},{4,8},{8,4},{12,0},{1,13},{5,9},{9,5},{13,1},{2,14},{6,10},... | collective-permute-start | bytes 147464 | tf_op jit(solution)/shard_map/ppermute | solution.py:236
  67.8 5.4 %collective-permute-start.22 = (bf16[8,3072]{1,0:T(8,128)(2,1)S(1)}, bf16[8,3072]{1,0:T(8,128)(2,1)S(1)}, u32[]{:S(2)}, u32[]{:S(2)}) collective-permute-start(bf16[8,3072]{1,0:T(8,128)(2,1)S(1)} %get-tuple-element.45), channel_id=1, source_target_pairs={{0,8},{4,12},{8,0},{12,4},{1,9},{5,13},{9,1},{13,5},{2,10},{6,14},... | collective-permute-start | bytes 147464 | tf_op jit(solution)/shard_map/ppermute | solution.py:236
  68.4 4.8 %collective-permute-start.23 = (bf16[8,3072]{1,0:T(8,128)(2,1)S(1)}, bf16[8,3072]{1,0:T(8,128)(2,1)S(1)}, u32[]{:S(2)}, u32[]{:S(2)}) collective-permute-start(bf16[8,3072]{1,0:T(8,128)(2,1)S(1)} %get-tuple-element.46), channel_id=1, source_target_pairs={{0,4},{4,0},{8,12},{12,8},{1,5},{5,1},{9,13},{13,9},{2,6},{6,2},{1... | collective-permute-start | bytes 147464 | tf_op jit(solution)/shard_map/ppermute | solution.py:236

commit v2 on v1

--- a/solution.py
+++ b/solution.py
@@ -255,12 +255,16 @@
     return cost(flops=STAGE_FLOPS)
 
 
+def doubled(x):
+    return jnp.concatenate([x] * max(1, 128 // x.shape[0]), axis=0)
+
+
 def params(limit):
     return pltpu.CompilerParams(vmem_limit_bytes=limit)
 
 
 MIB = 1 << 20
-STAGE_FLOPS = 8 * 10**9
+STAGE_FLOPS = 6 * 10**9
 EXPERT_MIB = 11
 
 
@@ -381,11 +385,11 @@
             floats = part_refs[k][...].astype(jnp.float32)
             factor = lax.rsqrt(jnp.mean(floats * floats, axis=-1, keepdims=True) + EPS)
             normed_ref[aligned(here ^ k, rows), :] = floats * factor * gain_ref[...]
-        normed = normed_ref[...].astype(jnp.bfloat16)
+        normed = doubled(normed_ref[...].astype(jnp.bfloat16))
         for i in range(columns // step):
             product = jnp.dot(
                 normed, weight_ref[:, i * step : (i + 1) * step], preferred_element_type=jnp.float32
-            )
+            )[:total]
             for at in range(0, step, HD):
                 head = (i * step + at) // HD
                 plain = product[:, at : at + HD]
@@ -504,10 +508,10 @@
         product = jnp.zeros((total, columns), jnp.float32)
         for k in range(ctx_count):
             product = product + jnp.dot(
-                attention_refs[k][:, :width],
+                doubled(attention_refs[k][:, :width]),
                 weight_ref[aligned(here ^ k, width), :],
                 preferred_element_type=jnp.float32,
-            )
+            )[:total]
         product = product.astype(jnp.bfloat16).astype(jnp.float32)
         out_ref[...] = (raw_ref[...] + product).astype(jnp.bfloat16)
 

time: 74 us -> 76.1 us (1.028)
  local copies, waits for them, and re-layouts: 1.12 us -> 3.36 us
    unnamed x46, local copies, waits for them, and re-layouts: 1.12 us -> 3.36 us
where the time goes in v2:
time: 76.1 us; the launch traced here: 75.9 us
  starting transfers between devices  30.1 us (40%)
  waiting for transfers between devices  24 us (32%)
  Pallas kernels  17.1 us (22%)
  local copies, waits for them, and re-layouts  3.36 us (4%)
  other arithmetic  0.89 us (1%)
    ppermute x20, starting transfers between devices, flip(): lax.ppermute(x, axis, [(i, i ^ mask) for i in range(lax.axis_size(axis))])  23.5 us
    ppermute x20, waiting for transfers between devices, flip(): lax.ppermute(x, axis, [(i, i ^ mask) for i in range(lax.axis_size(axis))])  19.9 us
    pallas_call x1, Pallas kernels, experts(): pl.pallas_call(kernel, out_shape=[pltpu.VMEM((slots, width), jnp.float32)...  12.9 us
    ppermute x3, waiting for transfers between devices, fast_layer(): arrived[shift] = lax.ppermute(payloads[shift], 'ctx', plan[2][shift])  4.04 us
    ppermute x3, starting transfers between devices, fast_layer(): arrived[shift] = lax.ppermute(payloads[shift], 'ctx', plan[2][shift])  3.55 us
    unnamed x46, local copies, waits for them, and re-layouts  3.36 us
    ppermute x1, starting transfers between devices, fast_layer(): one = lax.ppermute(packed[1], ('ctx', 'opt'), to_one)  3.08 us
  transfers between devices with their start and end apart: 24, of which 12 were waited for; matrix products, arithmetic and copies ran while one was open for 0% of the time, Pallas kernels for 2%

profile of v2, /device:TPU:0, one launch (start us, length us, event | category | flops | bytes accessed | tf_op | source)
XLA Modules:
  0.0 75.9 jit_solution(16393581787105781231)
XLA Ops:
  0.0 0.1 fusion.1
  0.2 0.1 pad_maximum_fusion
  0.3 0.0 copy-start.2
  0.3 1.0 %copy-done.2 = bf16[128,512]{1,0:T(8,128)(2,1)S(1)} copy-done((bf16[128,512]{1,0:T(8,128)(2,1)S(1)}, bf16[128,512]{1,0:T(8,128)(2,1)}, u32[]{:S(2)}) %copy-start.2) | copy-done | bytes 131096
  1.3 1.5 %copy-done.3 = bf16[128,512]{1,0:T(8,128)(2,1)S(1)} copy-done((bf16[128,512]{1,0:T(8,128)(2,1)S(1)}, bf16[128,512]{1,0:T(8,128)(2,1)}, u32[]{:S(2)}) %copy-start.3) | copy-done | bytes 131096
  2.8 0.7 copy-done.6
  3.5 0.1 pack.1
  3.6 3.1 %collective-permute-start.6 = (bf16[128,256]{1,0:T(8,128)(2,1)S(1)}, bf16[128,256]{1,0:T(8,128)(2,1)S(1)}, u32[]{:S(2)}, u32[]{:S(2)}) collective-permute-start(bf16[128,256]{1,0:T(8,128)(2,1)S(1)} %get-tuple-element.33), channel_id=1, source_target_pairs={{0,4},{1,9},{2,6},{3,11},{4,0},{5,13},{6,2},{7,15},{8,12},{9,1},{1... | collective-permute-start | bytes 196616 | tf_op jit(solution)/shard_map/ppermute | solution.py:768
  6.7 2.5 %collective-permute-start.2 = (bf16[8,3072]{1,0:T(8,128)(2,1)S(1)}, bf16[8,3072]{1,0:T(8,128)(2,1)S(1)}, u32[]{:S(2)}, u32[]{:S(2)}) collective-permute-start(bf16[8,3072]{1,0:T(8,128)(2,1)S(1)} %bitcast.15), channel_id=1, source_target_pairs={{0,12},{4,8},{8,4},{12,0},{1,13},{5,9},{9,5},{13,1},{2,14},{6,10},... | collective-permute-start | bytes 147464 | tf_op jit(solution)/shard_map/ppermute | solution.py:236
  9.2 0.1 collective-permute-start.1
  9.3 1.8 %collective-permute-start = (bf16[8,3072]{1,0:T(8,128)(2,1)S(1)}, bf16[8,3072]{1,0:T(8,128)(2,1)S(1)}, u32[]{:S(2)}, u32[]{:S(2)}) collective-permute-start(bf16[8,3072]{1,0:T(8,128)(2,1)S(1)} %bitcast.17), channel_id=1, source_target_pairs={{0,4},{4,0},{8,12},{12,8},{1,5},{5,1},{9,13},{13,9},{2,6},{6,2},{1... | collective-permute-start | bytes 147464 | tf_op jit(solution)/shard_map/ppermute | solution.py:236
  11.1 2.5 %collective-permute-start.8 = (bf16[64,256]{1,0:T(8,128)(2,1)S(1)}, bf16[64,256]{1,0:T(8,128)(2,1)S(1)}, u32[]{:S(2)}, u32[]{:S(2)}) collective-permute-start(bf16[64,256]{1,0:T(8,128)(2,1)S(1)} %get-tuple-element.34), channel_id=1, source_target_pairs={{0,12},{4,8},{8,4},{12,0},{1,13},{5,9},{9,5},{13,1},{2,14},{6,10},... | collective-permute-start | bytes 98312 | tf_op jit(solution)/shard_map/ppermute | solution.py:236
  13.6 0.0 collective-permute-done.6.refs_5_
  13.6 0.0 collective-permute-start.7
  13.6 0.0 collective-permute-done.2.refs_3_.refs_8_
  13.6 1.6 %collective-permute-done.1.refs_2_.refs_7_ = bf16[8,3072]{1,0:T(8,128)(2,1)S(1)} collective-permute-done((bf16[8,3072]{1,0:T(8,128)(2,1)S(1)}, bf16[8,3072]{1,0:T(8,128)(2,1)S(1)}, u32[]{:S(2)}, u32[]{:S(2)}) %collective-permute-start.1) | collective-permute-done | bytes 49184 | tf_op jit(solution)/shard_map/ppermute | solution.py:236
  15.2 0.0 collective-permute-done.refs_1_.refs_6_
  15.2 0.0 slice-start.15
  15.2 0.0 copy-start.4
  15.3 0.0 copy-start.5
  15.3 0.0 slice-start.6
  15.3 1.2 %project.1 = (bf16[32,1024]{1,0:T(8,128)(2,1)S(1)}, bf16[32,768]{1,0:T(8,128)(2,1)S(1)}, bf16[32,256]{1,0:T(8,128)(2,1)S(1)}, bf16[32,512]{1,0:T(8,128)(2,1)S(1)}) custom-call(bf16[8,3072]{1,0:T(8,128)(2,1)S(1)} %bitcast.18, bf16[8,3072]{1,0:T(8,128)(2,1)S(1)} %collective-permute-done.refs_1_.refs_6_, ...), custom_call_target="tpu_custom_call" | custom-call | bytes 6291456 | tf_op jit(solution)/shard_map/project/pallas_call | solution.py:408
  16.5 0.5 collective-permute-start.3
  17.0 2.5 %collective-permute-start.5 = (bf16[32,512]{1,0:T(8,128)(2,1)S(1)}, bf16[32,512]{1,0:T(8,128)(2,1)S(1)}, u32[]{:S(2)}, u32[]{:S(2)}) collective-permute-start(bf16[32,512]{1,0:T(8,128)(2,1)S(1)} %get-tuple-element.31), channel_id=1, source_target_pairs={{0,12},{4,8},{8,4},{12,0},{1,13},{5,9},{9,5},{13,1},{2,14},{6,10},... | collective-permute-start | bytes 98312 | tf_op jit(solution)/shard_map/ppermute | solution.py:774
  19.5 0.6 collective-permute-start.4
  20.1 4.0 %collective-permute-done.4.refs_2_ = bf16[32,256]{1,0:T(8,128)(2,1)S(1)} collective-permute-done((bf16[32,256]{1,0:T(8,128)(2,1)S(1)}, bf16[32,256]{1,0:T(8,128)(2,1)S(1)}, u32[]{:S(2)}, u32[]{:S(2)}) %collective-permute-start.4) | collective-permute-done | bytes 16416 | tf_op jit(solution)/shard_map/ppermute | solution.py:774
  24.1 0.0 slice-start
  24.1 0.0 slice-start.1
  24.1 0.0 slice-start.7
  24.2 0.0 slice-start.8
  24.2 1.0 %attend.1.refs_0_.refs_6_ = bf16[32,896]{1,0:T(8,128)(2,1)S(1)} custom-call(bf16[32,1024]{1,0:T(8,128)(2,1)S(1)} %get-tuple-element.28.refs_0_, bf16[32,768]{1,0:T(8,128)(2,1)S(1)} %collective-permute-done.3.refs_1_, bf16[32,256]{1,0:T(8,128)(2,1)S(1)} %collective-permute-done.4.refs_2_, bf16[32,512]{1,0:T(8,128)(2,1)S(1)} %collective-permute-done.5.refs_3_, ...), custom_call_target="tpu_custom_call" | custom-call | flops 6000000000 | tf_op jit(solution)/shard_map/attend/pallas_call | solution.py:483
  25.2 0.0 slice-start.2
  25.2 0.0 slice-start.3
  25.2 0.0 slice-start.9
  25.2 0.0 slice-start.10
  25.3 2.0 %collective-permute-start.12 = (bf16[32,896]{1,0:T(8,128)(2,1)S(1)}, bf16[32,896]{1,0:T(8,128)(2,1)S(1)}, u32[]{:S(2)}, u32[]{:S(2)}) collective-permute-start(bf16[32,896]{1,0:T(8,128)(2,1)S(1)} %attend.1.refs_0_.refs_6_), channel_id=1, source_target_pairs={{0,12},{4,8},{8,4},{12,0},{1,13},{5,9},{9,5},{13,1},{2,14},{6,10},... | collective-permute-start | bytes 172040 | tf_op jit(solution)/shard_map/ppermute | solution.py:236
  27.2 0.5 collective-permute-start.11
  27.7 2.0 %collective-permute-start.10 = (bf16[32,896]{1,0:T(8,128)(2,1)S(1)}, bf16[32,896]{1,0:T(8,128)(2,1)S(1)}, u32[]{:S(2)}, u32[]{:S(2)}) collective-permute-start(bf16[32,896]{1,0:T(8,128)(2,1)S(1)} %attend.1.refs_0_.refs_6_), channel_id=1, source_target_pairs={{0,4},{4,0},{8,12},{12,8},{1,5},{5,1},{9,13},{13,9},{2,6},{6,2},{1... | collective-permute-start | bytes 172040 | tf_op jit(solution)/shard_map/ppermute | solution.py:236
  29.7 1.8 %collective-permute-done.12.refs_3_.refs_9_ = bf16[32,896]{1,0:T(8,128)(2,1)S(1)} collective-permute-done((bf16[32,896]{1,0:T(8,128)(2,1)S(1)}, bf16[32,896]{1,0:T(8,128)(2,1)S(1)}, u32[]{:S(2)}, u32[]{:S(2)}) %collective-permute-start.12) | collective-permute-done | bytes 57376 | tf_op jit(solution)/shard_map/ppermute | solution.py:236
  31.5 1.5 %collective-permute-done.11.refs_2_.refs_8_ = bf16[32,896]{1,0:T(8,128)(2,1)S(1)} collective-permute-done((bf16[32,896]{1,0:T(8,128)(2,1)S(1)}, bf16[32,896]{1,0:T(8,128)(2,1)S(1)}, u32[]{:S(2)}, u32[]{:S(2)}) %collective-permute-start.11) | collective-permute-done | bytes 57376 | tf_op jit(solution)/shard_map/ppermute | solution.py:236
  33.0 0.8 %out_project.1.refs_0_ = bf16[32,768]{1,0:T(8,128)(2,1)S(1)} custom-call(bf16[32,896]{1,0:T(8,128)(2,1)S(1)} %attend.1.refs_0_.refs_6_, bf16[32,896]{1,0:T(8,128)(2,1)S(1)} %collective-permute-done.10.refs_1_.refs_7_, bf16[32,896]{1,0:T(8,128)(2,1)S(1)} %collective-permute-done.11.refs_2_.refs_8_, ...), custom_call_target="tpu_custom_call" | custom-call | flops 6000000000 | bytes 4718592 | tf_op jit(solution)/shard_map/out_project/pallas_call | solution.py:518
  33.8 2.0 %collective-permute-start.15 = (bf16[32,768]{1,0:T(8,128)(2,1)S(1)}, bf16[32,768]{1,0:T(8,128)(2,1)S(1)}, u32[]{:S(2)}, u32[]{:S(2)}) collective-permute-start(bf16[32,768]{1,0:T(8,128)(2,1)S(1)} %out_project.1.refs_0_), channel_id=1, source_target_pairs={{0,12},{4,8},{8,4},{12,0},{1,13},{5,9},{9,5},{13,1},{2,14},{6,10},... | collective-permute-start | bytes 147464 | tf_op jit(solution)/shard_map/ppermute | solution.py:236
  35.9 0.4 collective-permute-start.14
  36.2 2.0 %collective-permute-start.13 = (bf16[32,768]{1,0:T(8,128)(2,1)S(1)}, bf16[32,768]{1,0:T(8,128)(2,1)S(1)}, u32[]{:S(2)}, u32[]{:S(2)}) collective-permute-start(bf16[32,768]{1,0:T(8,128)(2,1)S(1)} %out_project.1.refs_0_), channel_id=1, source_target_pairs={{0,4},{4,0},{8,12},{12,8},{1,5},{5,1},{9,13},{13,9},{2,6},{6,2},{1... | collective-permute-start | bytes 147464 | tf_op jit(solution)/shard_map/ppermute | solution.py:236
  38.3 1.8 %collective-permute-done.15.refs_3_ = bf16[32,768]{1,0:T(8,128)(2,1)S(1)} collective-permute-done((bf16[32,768]{1,0:T(8,128)(2,1)S(1)}, bf16[32,768]{1,0:T(8,128)(2,1)S(1)}, u32[]{:S(2)}, u32[]{:S(2)}) %collective-permute-start.15) | collective-permute-done | bytes 49184 | tf_op jit(solution)/shard_map/ppermute | solution.py:236
  40.1 1.2 %collective-permute-done.14.refs_2_ = bf16[32,768]{1,0:T(8,128)(2,1)S(1)} collective-permute-done((bf16[32,768]{1,0:T(8,128)(2,1)S(1)}, bf16[32,768]{1,0:T(8,128)(2,1)S(1)}, u32[]{:S(2)}, u32[]{:S(2)}) %collective-permute-start.14) | collective-permute-done | bytes 49184 | tf_op jit(solution)/shard_map/ppermute | solution.py:236
  41.2 0.0 slice-start.4
  41.3 0.0 slice-start.11
  41.3 0.6 route.1
  41.9 1.6 %collective-permute-start.16 = (bf16[16,3072]{1,0:T(8,128)(2,1)S(1)}, bf16[16,3072]{1,0:T(8,128)(2,1)S(1)}, u32[]{:S(2)}, u32[]{:S(2)}) collective-permute-start(bf16[16,3072]{1,0:T(8,128)(2,1)S(1)} %get-tuple-element.38), channel_id=1, source_target_pairs={{0,2},{1,3},{2,0},{3,1},{4,6},{5,7},{6,4},{7,5},{8,10},{9,11},{10,... | collective-permute-start | bytes 294920 | tf_op jit(solution)/shard_map/ppermute | solution.py:236
  43.5 3.1 %collective-permute-done.16.refs_1_ = bf16[16,3072]{1,0:T(8,128)(2,1)S(1)} collective-permute-done((bf16[16,3072]{1,0:T(8,128)(2,1)S(1)}, bf16[16,3072]{1,0:T(8,128)(2,1)S(1)}, u32[]{:S(2)}, u32[]{:S(2)}) %collective-permute-start.16) | collective-permute-done | bytes 98336 | tf_op jit(solution)/shard_map/ppermute | solution.py:236
  46.6 1.3 %collective-permute-done.18.refs_3_ = bf16[16,3072]{1,0:T(8,128)(2,1)S(1)} collective-permute-done((bf16[16,3072]{1,0:T(8,128)(2,1)S(1)}, bf16[16,3072]{1,0:T(8,128)(2,1)S(1)}, u32[]{:S(2)}, u32[]{:S(2)}) %collective-permute-start.18) | collective-permute-done | bytes 98336 | tf_op jit(solution)/shard_map/ppermute | solution.py:236
  48.0 12.9 %experts.1 = (f32[16,3072]{1,0:T(8,128)S(1)}, f32[16,3072]{1,0:T(8,128)S(1)}, bf16[32,3072]{1,0:T(8,128)(2,1)S(1)}) custom-call(bf16[16,3072]{1,0:T(8,128)(2,1)S(1)} %get-tuple-element.37.refs_0_, bf16[16,3072]{1,0:T(8,128)(2,1)S(1)} %collective-permute-done.16.refs_1_, bf16[16,3072]{1,0:T(8,128)(2,1)S(1)} %collective-permute-done.17.refs_2_, ...), custom_call_target="tpu_custom_call" | custom-call | flops 4831838208 | bytes 75497472 | tf_op jit(solution)/shard_map/experts/pallas_call | solution.py:655
  60.9 0.2 collective-permute-start.19
  61.1 1.3 %collective-permute-done.19.core_ref = bf16[32,3072]{1,0:T(8,128)(2,1)S(1)} collective-permute-done((bf16[32,3072]{1,0:T(8,128)(2,1)S(1)}, bf16[32,3072]{1,0:T(8,128)(2,1)S(1)}, u32[]{:S(2)}, u32[]{:S(2)}) %collective-permute-start.19) | collective-permute-done | bytes 196640 | tf_op jit(solution)/shard_map/ppermute | solution.py:236
  62.4 1.5 %collective-permute-start.20 = (bf16[16,3072]{1,0:T(8,128)(2,1)S(1)}, bf16[16,3072]{1,0:T(8,128)(2,1)S(1)}, u32[]{:S(2)}, u32[]{:S(2)}) collective-permute-start(bf16[16,3072]{1,0:T(8,128)(2,1)S(1)} %merge.1), channel_id=1, source_target_pairs={{0,2},{1,3},{2,0},{3,1},{4,6},{5,7},{6,4},{7,5},{8,10},{9,11},{10,... | collective-permute-start | bytes 294920 | tf_op jit(solution)/shard_map/ppermute | solution.py:236
  64.0 3.4 %collective-permute-done.20.back_ref = bf16[16,3072]{1,0:T(8,128)(2,1)S(1)} collective-permute-done((bf16[16,3072]{1,0:T(8,128)(2,1)S(1)}, bf16[16,3072]{1,0:T(8,128)(2,1)S(1)}, u32[]{:S(2)}, u32[]{:S(2)}) %collective-permute-start.20) | collective-permute-done | bytes 98336 | tf_op jit(solution)/shard_map/ppermute | solution.py:236
  67.3 0.5 combine.1
  67.8 2.0 %collective-permute-start.21 = (bf16[8,3072]{1,0:T(8,128)(2,1)S(1)}, bf16[8,3072]{1,0:T(8,128)(2,1)S(1)}, u32[]{:S(2)}, u32[]{:S(2)}) collective-permute-start(bf16[8,3072]{1,0:T(8,128)(2,1)S(1)} %get-tuple-element.44), channel_id=1, source_target_pairs={{0,12},{4,8},{8,4},{12,0},{1,13},{5,9},{9,5},{13,1},{2,14},{6,10},... | collective-permute-start | bytes 147464 | tf_op jit(solution)/shard_map/ppermute | solution.py:236
  69.9 0.6 collective-permute-start.22
  70.5 1.8 %collective-permute-start.23 = (bf16[8,3072]{1,0:T(8,128)(2,1)S(1)}, bf16[8,3072]{1,0:T(8,128)(2,1)S(1)}, u32[]{:S(2)}, u32[]{:S(2)}) collective-permute-start(bf16[8,3072]{1,0:T(8,128)(2,1)S(1)} %get-tuple-element.46), channel_id=1, source_target_pairs={{0,4},{4,0},{8,12},{12,8},{1,5},{5,1},{9,13},{13,9},{2,6},{6,2},{1... | collective-permute-start | bytes 147464 | tf_op jit(solution)/shard_map/ppermute | solution.py:236
  72.3 1.7 %collective-permute-done.21 = bf16[8,3072]{1,0:T(8,128)(2,1)S(1)} collective-permute-done((bf16[8,3072]{1,0:T(8,128)(2,1)S(1)}, bf16[8,3072]{1,0:T(8,128)(2,1)S(1)}, u32[]{:S(2)}, u32[]{:S(2)}) %collective-permute-start.21) | collective-permute-done | bytes 49184 | tf_op jit(solution)/shard_map/ppermute | solution.py:236
  74.0 1.2 %collective-permute-done.22 = bf16[8,3072]{1,0:T(8,128)(2,1)S(1)} collective-permute-done((bf16[8,3072]{1,0:T(8,128)(2,1)S(1)}, bf16[8,3072]{1,0:T(8,128)(2,1)S(1)}, u32[]{:S(2)}, u32[]{:S(2)}) %collective-permute-start.22) | collective-permute-done | bytes 49184 | tf_op jit(solution)/shard_map/ppermute | solution.py:236
  75.2 0.7 fusion
  (48 shorter events, 0.1 us)
Async XLA Ops:
  0.0 6.7 %copy-start = (bf16[1,8,3072]{2,1,0:T(8,128)(2,1)S(1)}, bf16[1,8,3072]{2,1,0:T(8,128)(2,1)}, u32[]{:S(2)}) copy-start(bf16[1,8,3072]{2,1,0:T(8,128)(2,1)} %param.12) | copy-start | bytes 147460
  0.0 15.2 %slice-start.12 = ((s8[6291456]{0:T(1024)(128)(4,1)}), s8[2097152]{0:T(1024)(128)(4,1)S(1)}, s32[]{:S(2)}) async-start(s8[6291456]{0:T(1024)(128)(4,1)} %bitcast.13), calls=%async_computation.12 | async-start | bytes 4194304
  0.0 15.2 %copy-start.1 = (f32[3072]{0:T(1024)S(1)}, f32[3072]{0:T(1024)}, u32[]{:S(2)}) copy-start(f32[3072]{0:T(1024)} %param.15) | copy-start | bytes 36868
  0.3 15.0 %slice-start.13 = ((s8[6291456]{0:T(1024)(128)(4,1)}), s8[4194304]{0:T(1024)(128)(4,1)S(1)}, s32[]{:S(2)}) async-start(s8[6291456]{0:T(1024)(128)(4,1)} %bitcast.13), calls=%async_computation.13 | async-start | bytes 8388608
  0.3 1.1 %copy-start.2 = (bf16[128,512]{1,0:T(8,128)(2,1)S(1)}, bf16[128,512]{1,0:T(8,128)(2,1)}, u32[]{:S(2)}) copy-start(bf16[128,512]{1,0:T(8,128)(2,1)} %keys_ref.1) | copy-start | bytes 393220
  1.3 1.5 %copy-start.3 = (bf16[128,512]{1,0:T(8,128)(2,1)S(1)}, bf16[128,512]{1,0:T(8,128)(2,1)}, u32[]{:S(2)}) copy-start(bf16[128,512]{1,0:T(8,128)(2,1)} %values_ref.1) | copy-start | bytes 393220
  2.8 0.7 copy-start.6
  3.5 29.5 %slice-start.14 = ((s8[4718592]{0:T(1024)(128)(4,1)}), s8[4194304]{0:T(1024)(128)(4,1)S(1)}, s32[]{:S(2)}) async-start(s8[4718592]{0:T(1024)(128)(4,1)} %bitcast.21), calls=%async_computation.14 | async-start | bytes 8388608
  3.6 9.9 %collective-permute-start.6 = (bf16[128,256]{1,0:T(8,128)(2,1)S(1)}, bf16[128,256]{1,0:T(8,128)(2,1)S(1)}, u32[]{:S(2)}, u32[]{:S(2)}) collective-permute-start(bf16[128,256]{1,0:T(8,128)(2,1)S(1)} %get-tuple-element.33), channel_id=1, source_target_pairs={{0,4},{1,9},{2,6},{3,11},{4,0},{5,13},{6,2},{7,15},{8,12},{9,1},{1... | collective-permute-start | bytes 196616 | tf_op jit(solution)/shard_map/ppermute | solution.py:768
  6.7 6.9 %collective-permute-start.2 = (bf16[8,3072]{1,0:T(8,128)(2,1)S(1)}, bf16[8,3072]{1,0:T(8,128)(2,1)S(1)}, u32[]{:S(2)}, u32[]{:S(2)}) collective-permute-start(bf16[8,3072]{1,0:T(8,128)(2,1)S(1)} %bitcast.15), channel_id=1, source_target_pairs={{0,12},{4,8},{8,4},{12,0},{1,13},{5,9},{9,5},{13,1},{2,14},{6,10},... | collective-permute-start | bytes 147464 | tf_op jit(solution)/shard_map/ppermute | solution.py:236
  9.2 6.0 %collective-permute-start.1 = (bf16[8,3072]{1,0:T(8,128)(2,1)S(1)}, bf16[8,3072]{1,0:T(8,128)(2,1)S(1)}, u32[]{:S(2)}, u32[]{:S(2)}) collective-permute-start(bf16[8,3072]{1,0:T(8,128)(2,1)S(1)} %bitcast.16), channel_id=1, source_target_pairs={{0,8},{4,12},{8,0},{12,4},{1,9},{5,13},{9,1},{13,5},{2,10},{6,14},... | collective-permute-start | bytes 147464 | tf_op jit(solution)/shard_map/ppermute | solution.py:236
  9.3 5.9 %collective-permute-start = (bf16[8,3072]{1,0:T(8,128)(2,1)S(1)}, bf16[8,3072]{1,0:T(8,128)(2,1)S(1)}, u32[]{:S(2)}, u32[]{:S(2)}) collective-permute-start(bf16[8,3072]{1,0:T(8,128)(2,1)S(1)} %bitcast.17), channel_id=1, source_target_pairs={{0,4},{4,0},{8,12},{12,8},{1,5},{5,1},{9,13},{13,9},{2,6},{6,2},{1... | collective-permute-start | bytes 147464 | tf_op jit(solution)/shard_map/ppermute | solution.py:236
  11.1 5.9 %collective-permute-start.8 = (bf16[64,256]{1,0:T(8,128)(2,1)S(1)}, bf16[64,256]{1,0:T(8,128)(2,1)S(1)}, u32[]{:S(2)}, u32[]{:S(2)}) collective-permute-start(bf16[64,256]{1,0:T(8,128)(2,1)S(1)} %get-tuple-element.34), channel_id=1, source_target_pairs={{0,12},{4,8},{8,4},{12,0},{1,13},{5,9},{9,5},{13,1},{2,14},{6,10},... | collective-permute-start | bytes 98312 | tf_op jit(solution)/shard_map/ppermute | solution.py:236
  13.6 10.5 %collective-permute-start.7 = (bf16[128,256]{1,0:T(8,128)(2,1)S(1)}, bf16[128,256]{1,0:T(8,128)(2,1)S(1)}, u32[]{:S(2)}, u32[]{:S(2)}) collective-permute-start(bf16[128,256]{1,0:T(8,128)(2,1)S(1)} %collective-permute-done.6.refs_5_), channel_id=1, source_target_pairs={{0,1},{1,0},{2,3},{3,2},{4,5},{5,4},{6,7},{7,6},{8,9},{9,8},{10,11... | collective-permute-start | bytes 196616 | tf_op jit(solution)/shard_map/ppermute | solution.py:236
  15.2 17.8 %slice-start.15 = ((s8[4718592]{0:T(1024)(128)(4,1)}), s8[524288]{0:T(1024)(128)(4,1)S(1)}, s32[]{:S(2)}) async-start(s8[4718592]{0:T(1024)(128)(4,1)} %bitcast.21), calls=%async_computation.15 | async-start | bytes 1048576
  15.2 26.0 %copy-start.4 = (bf16[3072,8]{0,1:T(8,128)(2,1)S(1)}, bf16[3072,8]{0,1:T(8,128)(2,1)}, u32[]{:S(2)}) copy-start(bf16[3072,8]{0,1:T(8,128)(2,1)} %param.19) | copy-start | bytes 147460
  15.3 26.0 %copy-start.5 = (f32[3072]{0:T(1024)S(1)}, f32[3072]{0:T(1024)}, u32[]{:S(2)}) copy-start(f32[3072]{0:T(1024)} %param.16) | copy-start | bytes 36868
  15.3 32.6 %slice-start.6 = ((s8[25165824]{0:T(1024)(128)(4,1)}), s8[4194304]{0:T(1024)(128)(4,1)S(1)}, s32[]{:S(2)}) async-start(s8[25165824]{0:T(1024)(128)(4,1)} %bitcast.11), calls=%async_computation.6 | async-start | bytes 8388608
  16.5 7.6 %collective-permute-start.3 = (bf16[32,768]{1,0:T(8,128)(2,1)S(1)}, bf16[32,768]{1,0:T(8,128)(2,1)S(1)}, u32[]{:S(2)}, u32[]{:S(2)}) collective-permute-start(bf16[32,768]{1,0:T(8,128)(2,1)S(1)} %get-tuple-element.29), channel_id=1, source_target_pairs={{0,4},{4,0},{8,12},{12,8},{1,5},{5,1},{9,13},{13,9},{2,6},{6,2},{1... | collective-permute-start | bytes 147464 | tf_op jit(solution)/shard_map/ppermute | solution.py:774
  17.0 7.1 %collective-permute-start.9 = (bf16[64,256]{1,0:T(8,128)(2,1)S(1)}, bf16[64,256]{1,0:T(8,128)(2,1)S(1)}, u32[]{:S(2)}, u32[]{:S(2)}) collective-permute-start(bf16[64,256]{1,0:T(8,128)(2,1)S(1)} %collective-permute-done.8.refs_7_), channel_id=1, source_target_pairs={{0,1},{1,0},{2,3},{3,2},{4,5},{5,4},{6,7},{7,6},{8,9},{9,8},{10,11... | collective-permute-start | bytes 98312 | tf_op jit(solution)/shard_map/ppermute | solution.py:236
  17.0 7.1 %collective-permute-start.5 = (bf16[32,512]{1,0:T(8,128)(2,1)S(1)}, bf16[32,512]{1,0:T(8,128)(2,1)S(1)}, u32[]{:S(2)}, u32[]{:S(2)}) collective-permute-start(bf16[32,512]{1,0:T(8,128)(2,1)S(1)} %get-tuple-element.31), channel_id=1, source_target_pairs={{0,12},{4,8},{8,4},{12,0},{1,13},{5,9},{9,5},{13,1},{2,14},{6,10},... | collective-permute-start | bytes 98312 | tf_op jit(solution)/shard_map/ppermute | solution.py:774
  19.5 4.6 %collective-permute-start.4 = (bf16[32,256]{1,0:T(8,128)(2,1)S(1)}, bf16[32,256]{1,0:T(8,128)(2,1)S(1)}, u32[]{:S(2)}, u32[]{:S(2)}) collective-permute-start(bf16[32,256]{1,0:T(8,128)(2,1)S(1)} %get-tuple-element.30), channel_id=1, source_target_pairs={{0,8},{4,12},{8,0},{12,4},{1,9},{5,13},{9,1},{13,5},{2,10},{6,14},... | collective-permute-start | bytes 49160 | tf_op jit(solution)/shard_map/ppermute | solution.py:774
  24.1 23.8 %slice-start = ((s8[25165824]{0:T(1024)(128)(4,1)}), s8[4194304]{0:T(1024)(128)(4,1)S(1)}, s32[]{:S(2)}) async-start(s8[25165824]{0:T(1024)(128)(4,1)} %bitcast.9), calls=%async_computation | async-start | bytes 8388608
  24.1 23.8 %slice-start.1 = ((s8[25165824]{0:T(1024)(128)(4,1)}), s8[4194304]{0:T(1024)(128)(4,1)S(1)}, s32[]{:S(2)}) async-start(s8[25165824]{0:T(1024)(128)(4,1)} %bitcast.9), calls=%async_computation.1 | async-start | bytes 8388608
  24.1 23.8 %slice-start.7 = ((s8[25165824]{0:T(1024)(128)(4,1)}), s8[4194304]{0:T(1024)(128)(4,1)S(1)}, s32[]{:S(2)}) async-start(s8[25165824]{0:T(1024)(128)(4,1)} %bitcast.11), calls=%async_computation.7 | async-start | bytes 8388608
  24.2 23.7 %slice-start.8 = ((s8[25165824]{0:T(1024)(128)(4,1)}), s8[4194304]{0:T(1024)(128)(4,1)S(1)}, s32[]{:S(2)}) async-start(s8[25165824]{0:T(1024)(128)(4,1)} %bitcast.11), calls=%async_computation.8 | async-start | bytes 8388608
  25.2 22.7 %slice-start.2 = ((s8[25165824]{0:T(1024)(128)(4,1)}), s8[4194304]{0:T(1024)(128)(4,1)S(1)}, s32[]{:S(2)}) async-start(s8[25165824]{0:T(1024)(128)(4,1)} %bitcast.9), calls=%async_computation.2 | async-start | bytes 8388608
  25.2 22.7 %slice-start.3 = ((s8[25165824]{0:T(1024)(128)(4,1)}), s8[4194304]{0:T(1024)(128)(4,1)S(1)}, s32[]{:S(2)}) async-start(s8[25165824]{0:T(1024)(128)(4,1)} %bitcast.9), calls=%async_computation.3 | async-start | bytes 8388608
  25.2 22.7 %slice-start.9 = ((s8[25165824]{0:T(1024)(128)(4,1)}), s8[4194304]{0:T(1024)(128)(4,1)S(1)}, s32[]{:S(2)}) async-start(s8[25165824]{0:T(1024)(128)(4,1)} %bitcast.11), calls=%async_computation.9 | async-start | bytes 8388608
  25.2 22.7 %slice-start.10 = ((s8[25165824]{0:T(1024)(128)(4,1)}), s8[4194304]{0:T(1024)(128)(4,1)S(1)}, s32[]{:S(2)}) async-start(s8[25165824]{0:T(1024)(128)(4,1)} %bitcast.11), calls=%async_computation.10 | async-start | bytes 8388608
  25.3 6.2 %collective-permute-start.12 = (bf16[32,896]{1,0:T(8,128)(2,1)S(1)}, bf16[32,896]{1,0:T(8,128)(2,1)S(1)}, u32[]{:S(2)}, u32[]{:S(2)}) collective-permute-start(bf16[32,896]{1,0:T(8,128)(2,1)S(1)} %attend.1.refs_0_.refs_6_), channel_id=1, source_target_pairs={{0,12},{4,8},{8,4},{12,0},{1,13},{5,9},{9,5},{13,1},{2,14},{6,10},... | collective-permute-start | bytes 172040 | tf_op jit(solution)/shard_map/ppermute | solution.py:236
  27.2 5.8 %collective-permute-start.11 = (bf16[32,896]{1,0:T(8,128)(2,1)S(1)}, bf16[32,896]{1,0:T(8,128)(2,1)S(1)}, u32[]{:S(2)}, u32[]{:S(2)}) collective-permute-start(bf16[32,896]{1,0:T(8,128)(2,1)S(1)} %attend.1.refs_0_.refs_6_), channel_id=1, source_target_pairs={{0,8},{4,12},{8,0},{12,4},{1,9},{5,13},{9,1},{13,5},{2,10},{6,14},... | collective-permute-start | bytes 172040 | tf_op jit(solution)/shard_map/ppermute | solution.py:236
  27.7 5.3 %collective-permute-start.10 = (bf16[32,896]{1,0:T(8,128)(2,1)S(1)}, bf16[32,896]{1,0:T(8,128)(2,1)S(1)}, u32[]{:S(2)}, u32[]{:S(2)}) collective-permute-start(bf16[32,896]{1,0:T(8,128)(2,1)S(1)} %attend.1.refs_0_.refs_6_), channel_id=1, source_target_pairs={{0,4},{4,0},{8,12},{12,8},{1,5},{5,1},{9,13},{13,9},{2,6},{6,2},{1... | collective-permute-start | bytes 172040 | tf_op jit(solution)/shard_map/ppermute | solution.py:236
  33.8 6.3 %collective-permute-start.15 = (bf16[32,768]{1,0:T(8,128)(2,1)S(1)}, bf16[32,768]{1,0:T(8,128)(2,1)S(1)}, u32[]{:S(2)}, u32[]{:S(2)}) collective-permute-start(bf16[32,768]{1,0:T(8,128)(2,1)S(1)} %out_project.1.refs_0_), channel_id=1, source_target_pairs={{0,12},{4,8},{8,4},{12,0},{1,13},{5,9},{9,5},{13,1},{2,14},{6,10},... | collective-permute-start | bytes 147464 | tf_op jit(solution)/shard_map/ppermute | solution.py:236
  35.9 5.4 %collective-permute-start.14 = (bf16[32,768]{1,0:T(8,128)(2,1)S(1)}, bf16[32,768]{1,0:T(8,128)(2,1)S(1)}, u32[]{:S(2)}, u32[]{:S(2)}) collective-permute-start(bf16[32,768]{1,0:T(8,128)(2,1)S(1)} %out_project.1.refs_0_), channel_id=1, source_target_pairs={{0,8},{4,12},{8,0},{12,4},{1,9},{5,13},{9,1},{13,5},{2,10},{6,14},... | collective-permute-start | bytes 147464 | tf_op jit(solution)/shard_map/ppermute | solution.py:236
  36.2 5.0 %collective-permute-start.13 = (bf16[32,768]{1,0:T(8,128)(2,1)S(1)}, bf16[32,768]{1,0:T(8,128)(2,1)S(1)}, u32[]{:S(2)}, u32[]{:S(2)}) collective-permute-start(bf16[32,768]{1,0:T(8,128)(2,1)S(1)} %out_project.1.refs_0_), channel_id=1, source_target_pairs={{0,4},{4,0},{8,12},{12,8},{1,5},{5,1},{9,13},{13,9},{2,6},{6,2},{1... | collective-permute-start | bytes 147464 | tf_op jit(solution)/shard_map/ppermute | solution.py:236
  41.2 6.7 %slice-start.4 = ((s8[25165824]{0:T(1024)(128)(4,1)}), s8[4194304]{0:T(1024)(128)(4,1)S(1)}, s32[]{:S(2)}) async-start(s8[25165824]{0:T(1024)(128)(4,1)} %bitcast.9), calls=%async_computation.4 | async-start | bytes 8388608
  41.3 6.7 %slice-start.5 = ((s8[25165824]{0:T(1024)(128)(4,1)}), s8[4194304]{0:T(1024)(128)(4,1)S(1)}, s32[]{:S(2)}) async-start(s8[25165824]{0:T(1024)(128)(4,1)} %bitcast.9), calls=%async_computation.5 | async-start | bytes 8388608
  41.3 6.7 %slice-start.11 = ((s8[25165824]{0:T(1024)(128)(4,1)}), s8[4194304]{0:T(1024)(128)(4,1)S(1)}, s32[]{:S(2)}) async-start(s8[25165824]{0:T(1024)(128)(4,1)} %bitcast.11), calls=%async_computation.11 | async-start | bytes 8388608
  41.9 4.7 %collective-permute-start.16 = (bf16[16,3072]{1,0:T(8,128)(2,1)S(1)}, bf16[16,3072]{1,0:T(8,128)(2,1)S(1)}, u32[]{:S(2)}, u32[]{:S(2)}) collective-permute-start(bf16[16,3072]{1,0:T(8,128)(2,1)S(1)} %get-tuple-element.38), channel_id=1, source_target_pairs={{0,2},{1,3},{2,0},{3,1},{4,6},{5,7},{6,4},{7,5},{8,10},{9,11},{10,... | collective-permute-start | bytes 294920 | tf_op jit(solution)/shard_map/ppermute | solution.py:236
  43.5 3.1 %collective-permute-start.17 = (bf16[16,3072]{1,0:T(8,128)(2,1)S(1)}, bf16[16,3072]{1,0:T(8,128)(2,1)S(1)}, u32[]{:S(2)}, u32[]{:S(2)}) collective-permute-start(bf16[16,3072]{1,0:T(8,128)(2,1)S(1)} %get-tuple-element.37.refs_0_), channel_id=1, source_target_pairs={{0,1},{1,0},{2,3},{3,2},{4,5},{5,4},{6,7},{7,6},{8,9},{9,8},{10,11... | collective-permute-start | bytes 294920 | tf_op jit(solution)/shard_map/ppermute | solution.py:236
  46.6 1.3 %collective-permute-start.18 = (bf16[16,3072]{1,0:T(8,128)(2,1)S(1)}, bf16[16,3072]{1,0:T(8,128)(2,1)S(1)}, u32[]{:S(2)}, u32[]{:S(2)}) collective-permute-start(bf16[16,3072]{1,0:T(8,128)(2,1)S(1)} %collective-permute-done.16.refs_1_), channel_id=1, source_target_pairs={{0,1},{1,0},{2,3},{3,2},{4,5},{5,4},{6,7},{7,6},{8,9},{9,8},{10,11... | collective-permute-start | bytes 294920 | tf_op jit(solution)/shard_map/ppermute | solution.py:236
  60.9 1.5 %collective-permute-start.19 = (bf16[32,3072]{1,0:T(8,128)(2,1)S(1)}, bf16[32,3072]{1,0:T(8,128)(2,1)S(1)}, u32[]{:S(2)}, u32[]{:S(2)}) collective-permute-start(bf16[32,3072]{1,0:T(8,128)(2,1)S(1)} %get-tuple-element.40), channel_id=1, source_target_pairs={{0,1},{1,0},{2,3},{3,2},{4,5},{5,4},{6,7},{7,6},{8,9},{9,8},{10,11... | collective-permute-start | bytes 589832 | tf_op jit(solution)/shard_map/ppermute | solution.py:236
  62.4 4.9 %collective-permute-start.20 = (bf16[16,3072]{1,0:T(8,128)(2,1)S(1)}, bf16[16,3072]{1,0:T(8,128)(2,1)S(1)}, u32[]{:S(2)}, u32[]{:S(2)}) collective-permute-start(bf16[16,3072]{1,0:T(8,128)(2,1)S(1)} %merge.1), channel_id=1, source_target_pairs={{0,2},{1,3},{2,0},{3,1},{4,6},{5,7},{6,4},{7,5},{8,10},{9,11},{10,... | collective-permute-start | bytes 294920 | tf_op jit(solution)/shard_map/ppermute | solution.py:236
  67.8 6.2 %collective-permute-start.21 = (bf16[8,3072]{1,0:T(8,128)(2,1)S(1)}, bf16[8,3072]{1,0:T(8,128)(2,1)S(1)}, u32[]{:S(2)}, u32[]{:S(2)}) collective-permute-start(bf16[8,3072]{1,0:T(8,128)(2,1)S(1)} %get-tuple-element.44), channel_id=1, source_target_pairs={{0,12},{4,8},{8,4},{12,0},{1,13},{5,9},{9,5},{13,1},{2,14},{6,10},... | collective-permute-start | bytes 147464 | tf_op jit(solution)/shard_map/ppermute | solution.py:236
  69.9 5.4 %collective-permute-start.22 = (bf16[8,3072]{1,0:T(8,128)(2,1)S(1)}, bf16[8,3072]{1,0:T(8,128)(2,1)S(1)}, u32[]{:S(2)}, u32[]{:S(2)}) collective-permute-start(bf16[8,3072]{1,0:T(8,128)(2,1)S(1)} %get-tuple-element.45), channel_id=1, source_target_pairs={{0,8},{4,12},{8,0},{12,4},{1,9},{5,13},{9,1},{13,5},{2,10},{6,14},... | collective-permute-start | bytes 147464 | tf_op jit(solution)/shard_map/ppermute | solution.py:236
  70.5 4.8 %collective-permute-start.23 = (bf16[8,3072]{1,0:T(8,128)(2,1)S(1)}, bf16[8,3072]{1,0:T(8,128)(2,1)S(1)}, u32[]{:S(2)}, u32[]{:S(2)}) collective-permute-start(bf16[8,3072]{1,0:T(8,128)(2,1)S(1)} %get-tuple-element.46), channel_id=1, source_target_pairs={{0,4},{4,0},{8,12},{12,8},{1,5},{5,1},{9,13},{13,9},{2,6},{6,2},{1... | collective-permute-start | bytes 147464 | tf_op jit(solution)/shard_map/ppermute | solution.py:236
